TPU v7x, 32 devices: a whole 2x2x4 slice. The times are simulated.
32 devices in a mesh: lat: 8 (over y, x, core), chan: 4 (over z).
Axes of the slice: x: 2, y: 2, z: 4, core: 2. Of those that a mesh axis runs over, the one named last changes fastest.
Arguments:
- atmosphere: bfloat16 [256, 64, 1536], P('chan', 'lat'), may hold values from -6 to 6
- first_weight: bfloat16 [256, 16, 5, 5], P('chan'), may hold values from -0.3125 to 0.3125
- first_bias: float32 [256], P('chan'), may hold values from -3 to 3
- second_weight: bfloat16 [256, 16, 5, 5], P('chan'), may hold values from -0.3125 to 0.3125
Outputs:
- spectrum: float32 [128, 2, 256, 2, 128], P('lat', None, 'chan')
All inputs are finite; a program needn't handle non-finite values.
Results may differ from a plain program's by a relative error of at most 0.007.
Values may be sent and summed in bfloat16 or wider, within the bound.
No kernel may reach another device: no remote copies, remote signals or barrier semaphores. Data moves between devices by JAX's collectives and lax.ppermute only.
A program may use at most 128 MiB of HBM per device.

v0:
```python
import math

import jax
import jax.numpy as jnp
from jax import lax
from jax.sharding import PartitionSpec as P

ORDERS = 128
DEGREES = 256


def extended_2(shard, sides, width):
    for axis, dim in sides:
        devices, length = (lax.axis_size(axis), shard.shape[dim])
        up = [(i, (i + 1) % devices) for i in range(devices - 1)]
        down = [(j, i) for i, j in up]
        last = lax.slice_in_dim(shard, length - width, length, axis=dim)
        initial = lax.slice_in_dim(shard, 0, width, axis=dim)
        before = lax.ppermute(last, axis, up)
        after = lax.ppermute(initial, axis, down)
        shard = jnp.concatenate([before, shard, after], axis=dim)
    return shard


def partner(value, axis, apart):
    mask = 2**apart
    pairs = [(source, source ^ mask) for source in range(lax.axis_size(axis))]
    return lax.ppermute(value, axis, pairs)


def fourier_table(length, orders):
    places = lax.broadcasted_iota(jnp.int32, (length, orders), 0)
    numbers = lax.broadcasted_iota(jnp.int32, (length, orders), 1) + 1
    phases = (places * numbers % length).astype(jnp.float32) * (2.0 * math.pi / length)
    factor = 1.0 / math.sqrt(length)
    return (jnp.concatenate([jnp.cos(phases), -jnp.sin(phases)], axis=1) * factor).astype(
        jnp.bfloat16
    )


def legendre(colatitude, orders, degrees):
    cosine = jnp.cos(colatitude)[None, :]
    sines = jnp.sin(colatitude)[None, :]
    order_real = orders.astype(jnp.float32)[:, None]
    log_diag = 0.5 * (
        jnp.log((2.0 * order_real + 1.0) / 2.0)
        + lax.lgamma(2.0 * order_real + 1.0)
        - order_real * math.log(4.0)
        - 2.0 * lax.lgamma(order_real + 1.0)
    ) + order_real * jnp.log(sines)
    diagonal = jnp.exp(log_diag)
    empty_rows = jnp.zeros_like(diagonal)

    def advance(carried, degree):
        latest, before = carried
        degree_real = degree.astype(jnp.float32)
        spread = jnp.maximum(degree_real * degree_real - order_real * order_real, 1.0)
        raising = jnp.sqrt(jnp.maximum(4.0 * degree_real * degree_real - 1.0, 1.0) / spread)
        previous = degree_real - 1.0
        lowering = jnp.sqrt(
            jnp.maximum(previous * previous - order_real * order_real, 0.0)
            / jnp.maximum(4.0 * previous * previous - 1.0, 1.0)
        )
        raised = raising * (cosine * latest - lowering * before)
        result = jnp.where(
            degree_real == order_real, diagonal, jnp.where(degree_real > order_real, raised, 0.0)
        )
        return ((result, latest), result)

    _, stacked = lax.scan(
        advance, (empty_rows, empty_rows), jnp.arange(degrees, dtype=jnp.int32), unroll=16
    )
    return stacked


def weighted_table(north_rows, orders, total_rows, degrees):
    colatitude = math.pi * (north_rows.astype(jnp.float32) + 0.5) / total_rows
    quadrature = math.pi * jnp.sin(colatitude) / math.sqrt(total_rows)
    return legendre(colatitude, orders, degrees) * quadrature[None, None, :]


def project(even_sum, odd_sum, stacked, orders):
    degrees, number, height = stacked.shape
    paired = (
        stacked.reshape(degrees // 2, 2, number, height).transpose(2, 1, 3, 0).astype(jnp.bfloat16)
    )
    parity = (orders[:, None] + jnp.arange(2, dtype=jnp.int32)[None, :]) % 2 == 0
    selected = jnp.where(parity, even_sum[..., None], odd_sum[..., None])
    return jnp.einsum("crakq,kqrj->kqcaj", selected, paired, preferred_element_type=jnp.float32)


def convolve(padded, kernel):
    radius = kernel.shape[3] // 2
    widened = jnp.concatenate([padded[..., -radius:], padded, padded[..., :radius]], axis=2)
    result = lax.conv_general_dilated(
        widened[None],
        kernel,
        (1, 1),
        "VALID",
        feature_group_count=padded.shape[0] // kernel.shape[1],
        preferred_element_type=jnp.float32,
    )
    return result[0]


def extend(grid_field, rim_width):
    return extended_2(grid_field, (("lat", 1),), rim_width)


def per_device(atmosphere, first_weight, first_bias, second_weight):
    members = lax.axis_size("lat")
    halfway = members // 2
    position = lax.axis_index("lat")
    southern = position >= halfway
    band_rows = atmosphere.shape[1]
    circle = atmosphere.shape[2]
    radius = first_weight.shape[3] // 2
    offsets = first_bias[:, None, None]
    extended = extend(atmosphere, radius)
    hidden = jax.nn.gelu(convolve(extended, first_weight) + offsets, approximate=False).astype(
        jnp.bfloat16
    )
    updated = atmosphere.astype(jnp.float32) + convolve(extend(hidden, radius), second_weight)
    updated = updated.astype(jnp.bfloat16)
    fourier = fourier_table(circle, ORDERS)
    spectra = jnp.dot(updated.reshape(-1, circle), fourier, preferred_element_type=jnp.float32)
    spectra = spectra.astype(jnp.bfloat16).reshape(atmosphere.shape[0], band_rows, 2, ORDERS)
    half_rows = band_rows // 2
    leading = spectra[:, :half_rows]
    incoming = spectra[:, half_rows:]
    for bit in range(members.bit_length() - 1):
        incoming = partner(incoming, "lat", bit)
    north_part = jnp.where(southern, incoming, leading).astype(jnp.float32)
    south_part = jnp.where(southern, leading[:, ::-1], incoming[:, ::-1]).astype(jnp.float32)
    even_sum = (north_part + south_part).astype(jnp.bfloat16)
    odd_sum = (north_part - south_part).astype(jnp.bfloat16)
    total_rows = band_rows * members
    owned_count = ORDERS // members
    places = jnp.arange(half_rows * members, dtype=jnp.int32)
    device = places // half_rows
    south_side = device >= halfway
    band_number = jnp.where(south_side, members - 1 - device, device)
    north_rows = band_number * band_rows + jnp.where(south_side, half_rows, 0) + places % half_rows
    owned_orders = position * owned_count + 1 + jnp.arange(owned_count, dtype=jnp.int32)
    spherical_owned = weighted_table(north_rows, owned_orders, total_rows, DEGREES)
    return project(
        lax.all_to_all(even_sum, "lat", split_axis=3, concat_axis=1, tiled=True),
        lax.all_to_all(odd_sum, "lat", split_axis=3, concat_axis=1, tiled=True),
        spherical_owned,
        owned_orders,
    )


def solution(mesh):
    placed = (
        P("chan", "lat", None),
        P("chan", None, None, None),
        P("chan"),
        P("chan", None, None, None),
    )
    return jax.shard_map(
        per_device,
        mesh=mesh,
        in_specs=placed,
        out_specs=P("lat", None, "chan", None, None),
        check_vma=False,
    )
```

profile of v0, /device:TPU:0, one launch (start us, length us, event | category | flops | bytes accessed | tf_op | source)
XLA Modules:
  0.0 2871.3 jit_solution(14951439106316437851)
XLA Ops:
  0.0 2.6 fusion.110
  2.7 3.2 collective-permute-start
  5.9 1.3 collective-permute-start.1
  7.2 0.2 copy.108
  7.5 1.0 copy.111
  8.5 0.5 iota_add_fusion.1
  9.0 1.0 constant_dynamic-update-slice_fusion.18
  10.0 0.5 constant_dynamic-update-slice_fusion.17
  10.5 0.4 collective-permute-done.1
  10.9 0.1 fusion.108
  11.0 1.3 copy-done.1
  12.3 4.6 concatenate.23
  16.9 69.6 %copy.88 = bf16[1,4,16,12,1540]{2,0,1,4,3:T(2,128)(2,1)} copy(bf16[1,4,16,12,1540]{4,2,1,3,0:T(8,128)(2,1)S(1)} %bitcast.358) | data formatting | bytes 4730880 | tf_op jit(solution)/shard_map/broadcast_in_dim | solution.py:96
  86.5 1176.9 %fusion.112 = f32[1,4,16,8,1536]{2,0,1,4,3:T(1,128)} fusion(bf16[1,4,16,12,1540]{2,0,1,4,3:T(2,128)(2,1)} %copy.88, bf16[4,16,16,5,5]{2,1,0,4,3:T(8,128)(2,1)S(1)} %bitcast.369), kind=kOutput, calls=%fused_computation.252 | convolution fusion | flops 629145600 | bytes 5562368 | tf_op jit(solution)/shard_map/conv_general_dilated | solution.py:95
  1263.5 30.4 %copy.90 = f32[1,4,16,8,1536]{4,3,2,1,0:T(8,128)S(1)} copy(f32[1,4,16,8,1536]{2,0,1,4,3:T(1,128)} %fusion.112) | data formatting | bytes 6291456 | tf_op jit(solution)/shard_map/conv_general_dilated | solution.py:95
  1293.9 7.5 fusion.37
  1301.5 0.5 fusion.109
  1302.0 9.3 collective-permute-start.2
  1311.3 1.3 collective-permute-start.3
  1312.6 4.4 fusion.61
  1317.0 2.0 pad_maximum_fusion
  1319.0 0.9 fusion.107
  1319.8 6.1 concatenate.25
  1325.9 71.0 %copy.92 = bf16[1,4,16,12,1540]{2,0,1,4,3:T(2,128)(2,1)} copy(bf16[1,4,16,12,1540]{4,3,2,1,0:T(8,128)(2,1)} %bitcast.357) | data formatting | bytes 4730880 | tf_op jit(solution)/shard_map/broadcast_in_dim | solution.py:96
  1396.9 1195.3 %fusion.113 = f32[1,4,16,8,1536]{2,0,1,4,3:T(1,128)} fusion(bf16[1,4,16,12,1540]{2,0,1,4,3:T(2,128)(2,1)} %copy.92, bf16[4,16,16,5,5]{2,1,0,4,3:T(8,128)(2,1)S(1)} %bitcast.368), kind=kOutput, calls=%fused_computation.253 | convolution fusion | flops 629145600 | bytes 5562368 | tf_op jit(solution)/shard_map/conv_general_dilated | solution.py:95
  2592.2 30.4 %copy.94 = f32[1,4,16,8,1536]{4,3,2,1,0:T(8,128)S(1)} copy(f32[1,4,16,8,1536]{2,0,1,4,3:T(1,128)} %fusion.113) | data formatting | bytes 6291456 | tf_op jit(solution)/shard_map/conv_general_dilated | solution.py:95
  2622.7 2.1 fusion.38
  2624.8 0.6 fusion.52
  2625.6 5.5 collective-permute-start.4
  2631.0 1.0 collective-permute-done.4
  2632.0 0.9 collective-permute-start.5
  2633.0 4.8 collective-permute-done.5
  2637.9 4.8 collective-permute-done.6
  2642.8 0.2 copy.97
  2643.0 0.9 reshape.1376
  2643.9 3.4 all-to-all-start
  2647.3 209.0 %while.21 = (s32[]{:T(128)}, f32[16,32]{1,0:T(8,128)S(1)}, f32[16,32]{1,0:T(8,128)S(1)}, f32[16,16,16,32]{3,2,1,0:T(8,128)S(1)}, s32[16,16]{1,0:T(8,128)S(1)}, /...) while((s32[]{:T(128)}, f32[16,32]{1,0:T(8,128)S(1)}, ...), condition=%wide.region_1.2_spmd.clone.clone.clone.clone, body=%wide.region_0.1_spmd.clone.clone.clone.clone.sunk | while | flops 120962 | bytes 856251 | solution.py:70
  2647.3 0.7 fusion.120
  2652.4 0.1 constant_dynamic-update-slice_fusion.39
  2660.4 0.7 fusion.120
  2665.5 0.1 constant_dynamic-update-slice_fusion.39
  2673.5 0.7 fusion.120
  2686.5 0.7 fusion.120
  2699.6 0.7 fusion.120
  2712.6 0.7 fusion.120
  2725.7 0.7 fusion.120
  2738.8 0.7 fusion.120
  2751.8 0.7 fusion.120
  2764.9 0.7 fusion.120
  2778.0 0.7 fusion.120
  2791.0 0.7 fusion.120
  2804.1 0.7 fusion.120
  2817.2 0.7 fusion.120
  2830.2 0.7 fusion.120
  2843.3 0.7 fusion.120
  2856.3 0.2 copy.101
  2856.5 0.9 reshape.1374
  2857.4 4.1 all-to-all-start.1
  2861.6 1.3 copy.105
  2862.9 0.2 reshape.1377
  2863.3 3.7 all-to-all-done.1
  2867.0 0.2 reshape.1375
  2867.4 0.6 fusion.63
  2868.0 3.0 copy.106
  (858 shorter events, 31.5 us)
Async XLA Ops:
  0.0 10.0 copy-start
  0.0 7.2 copy-start.5
  0.0 7.5 copy-start.6
  2.7 6.3 collective-permute-start
  5.9 4.9 collective-permute-start.1
  10.9 1.4 copy-start.1
  1263.4 30.4 %copy-start.7 = (f32[64]{0:T(128)S(1)}, f32[64]{0:T(128)}, u32[]{:S(2)}) copy-start(f32[64]{0:T(128)} %param.8) | copy-start | bytes 772
  1293.9 18.7 copy-start.8
  1302.0 15.0 collective-permute-start.2
  1311.3 5.7 collective-permute-start.3
  1325.9 71.0 %copy-start.4 = (bf16[64,16,5,5]{1,0,3,2:T(8,128)(2,1)S(1)}, bf16[64,16,5,5]{1,0,3,2:T(8,128)(2,1)}, u32[]{:S(2)}) copy-start(bf16[64,16,5,5]{1,0,3,2:T(8,128)(2,1)} %copy.111) | copy-start | bytes 153604
  2622.7 2.2 copy-start.2
  2622.7 2.2 copy-start.3
  2625.6 6.5 collective-permute-start.4
  2632.0 5.8 collective-permute-start.5
  2637.8 5.0 collective-permute-start.6
  2643.9 213.5 %all-to-all-start = ((bf16[8,2,4096]{2,1,0:T(2,128)(2,1)}), bf16[8,2,4096]{2,1,0:T(2,128)(2,1)S(1)}, u32[]{:S(2)}, u32[]{:S(2)}) async-start(bf16[8,2,4096]{2,1,0:T(2,128)(2,1)} %reshape.1376), calls=%async_computation | async-start | bytes 262144 | tf_op jit(solution)/shard_map/all_to_all | solution.py:147
  2857.4 9.6 all-to-all-start.1
where the time goes:
time: 2890 us; the launch traced here: 2870 us
  matrix products  2370 us (82%)
  local copies, waits for them, and re-layouts  239 us (8%)
  loops' own time  167 us (6%)
  other arithmetic  47.2 us (2%)
  starting transfers between devices  29 us (1%)
    conv_general_dilated x2, matrix products, convolve(): lax.conv_general_dilated(widened[None], kernel, (1, 1), 'VALID', feature_...  2370 us
    another operation x1, loops' own time, legendre(): lax.scan(advance, (empty_rows, empty_rows), jnp.arange(degrees, dtype=jnp...  167 us
    broadcast_in_dim x2, local copies, waits for them, and re-layouts, convolve(): widened[None]  141 us
    conv_general_dilated x2, local copies, waits for them, and re-layouts, convolve(): lax.conv_general_dilated(widened[None], kernel, (1, 1), 'VALID', feature_...  60.8 us
  transfers between devices with their start and end apart: 9, of which 5 were waited for; matrix products, arithmetic and copies ran while one was open for 2% of the time, Pallas kernels for 0%

commit v1 on v0

v1 whole, which is shorter than its diff:
```python
import math

import jax
import jax.numpy as jnp
import numpy as np
from jax import lax
from jax.experimental import pallas as pl
from jax.experimental.pallas import tpu as pltpu
from jax.sharding import PartitionSpec as P

ORDERS = 128
DEGREES = 256
VMEM_BYTES = 40 * 2**20
LANES = 128
F32 = jnp.float32
BF16 = jnp.bfloat16


def dot_tn(left, right):
    return lax.dot_general(left, right, (((0,), (0,)), ((), ())), preferred_element_type=F32)


def dot_nt(left, right):
    return lax.dot_general(left, right, (((1,), (1,)), ((), ())), preferred_element_type=F32)


def dot_nn(left, right):
    return jnp.dot(left, right, preferred_element_type=F32)


def iota(shape, dim):
    return lax.broadcasted_iota(jnp.int32, shape, dim)


def gelu(value):
    return 0.5 * value * (1.0 + lax.erf(value * math.sqrt(0.5)))


def call(kernel, name, out_shape, scratch, flops, args, grid=None, in_specs=None, out_specs=None):
    whole = pl.BlockSpec(memory_space=pltpu.VMEM)
    extra = {} if grid is None else {"grid": grid}
    size = sum(math.prod(a.shape) * a.dtype.itemsize for a in (*args, *jax.tree.leaves(out_shape)))
    return pl.pallas_call(
        kernel,
        out_shape=out_shape,
        in_specs=in_specs or [whole] * len(args),
        out_specs=out_specs or jax.tree.map(lambda _: whole, out_shape),
        scratch_shapes=scratch,
        compiler_params=pltpu.CompilerParams(vmem_limit_bytes=VMEM_BYTES),
        cost_estimate=pl.CostEstimate(flops=flops, transcendentals=0, bytes_accessed=size),
        name=name,
        **extra,
    )(*args)


def turned(number, length):
    number = number.astype(F32)
    number = number - length * jnp.floor(number / length)
    return number * (2.0 * math.pi / length)


def write_fourier(fourier_ref, length, orders):
    tile = 128
    factor = 1.0 / math.sqrt(length)
    shape = (tile, orders)
    fine = turned(iota(shape, 0) * (iota(shape, 1) + 1), length)
    fine_cos, fine_sin = jnp.cos(fine), jnp.sin(fine)
    blocks = length // tile
    padded = -(-blocks // 8) * 8
    shape = (padded, orders)
    coarse = turned(iota(shape, 0) * tile * (iota(shape, 1) + 1), length)
    coarse_cos, coarse_sin = jnp.cos(coarse) * factor, jnp.sin(coarse) * factor
    for block in range(blocks):
        cosine = coarse_cos[block : block + 1, :]
        sine = coarse_sin[block : block + 1, :]
        rows = slice(block * tile, (block + 1) * tile)
        fourier_ref[rows, :orders] = (cosine * fine_cos - sine * fine_sin).astype(BF16)
        fourier_ref[rows, orders:] = (-(sine * fine_cos + cosine * fine_sin)).astype(BF16)


def write_spectra(send_ref, slot, real, imaginary):
    members, _, owned, _ = send_ref.shape
    flipped = jnp.concatenate([real, imaginary], axis=0).T
    for device in range(members):
        send_ref[device, slot] = flipped[device * owned : (device + 1) * owned, :].astype(BF16)


def taps_of(weight_ref, dx):
    return jnp.concatenate([weight_ref[dy, dx] for dy in range(weight_ref.shape[0])], axis=0)


def shifted_sum(partial_ref, rows, height, first, count):
    taps = rows // height
    radius = taps // 2
    total = None
    for dx in range(taps):
        start = dx * height + first
        piece = partial_ref[start : start + count, :]
        if dx != radius:
            piece = pltpu.roll(piece, (radius - dx) % piece.shape[1], 1)
        total = piece if total is None else total + piece
    return total


def interior_kernel(
    group, weight_ref, bias_ref, field_ref,
    edge_ref, rim_ref, fourier_ref, send_field_ref, send_hidden_ref,
    band_ref, partial_ref, hidden_ref, spectra_ref,
):
    taps = weight_ref.shape[0]
    radius = taps // 2
    channels = weight_ref.shape[3]
    groups = channels // group
    length = field_ref.shape[1]
    height = field_ref.shape[0] // channels
    orders = fourier_ref.shape[1] // 2
    inner = height - 2 * radius
    block = height * group
    rows = taps * block

    write_fourier(fourier_ref, length, orders)
    shape = (taps * group, height * block)
    place = iota(shape, 0)
    column = iota(shape, 1)
    out_row, column = column // block, column % block
    chosen = (place % group == column // height) & (place // group == column % height - out_row + radius)
    selector = chosen.astype(F32).astype(BF16)
    rim_shape = (taps * group, radius * group)
    rim_place = iota(rim_shape, 0)
    rim_column = iota(rim_shape, 1)
    same = rim_place % group == rim_column // radius
    rim_row = rim_column % radius
    rim_rows = taps * radius * group
    for dx in range(taps):
        mine = taps_of(weight_ref, dx)
        spread = dot_tn(mine, selector).astype(BF16)
        for g in range(groups):
            for row in range(height):
                start = g * rows + dx * block + row * group
                band_ref[start : start + group, :] = spread[
                    g * group : (g + 1) * group, row * block : (row + 1) * block
                ]
        for side in range(2):
            for row in range(radius):
                tap = rim_row - row + (0 if side == 0 else taps - 1)
                pick = (same & (rim_place // group == tap)).astype(F32).astype(BF16)
                spread = dot_tn(mine, pick).astype(BF16)
                for g in range(groups):
                    start = (g * 2 + side) * rim_rows + (dx * radius + row) * group
                    rim_ref[start : start + group, :] = spread[g * group : (g + 1) * group, :]

    def per_group(g, carry):
        band = band_ref[pl.ds(pl.multiple_of(g * rows, 16), rows), :]
        field = field_ref[pl.ds(pl.multiple_of(g * block, 16), block), :]
        partial_ref[...] = dot_nn(band, field)
        mine = pl.ds(pl.multiple_of(g * group, 16), group)
        bias = bias_ref[mine, :][:, :1]
        for row in range(height):
            total = shifted_sum(partial_ref, rows, block, row * group, group) + bias
            if radius <= row < height - radius:
                start = pl.multiple_of((row - radius) * channels + g * group, 16)
                hidden_ref[pl.ds(start, group), :] = gelu(total).astype(BF16)
            else:
                edge_ref[row if row < radius else row - inner, mine, :] = total
        return carry

    lax.fori_loop(0, groups, per_group, 0)

    found = dot_nn(field_ref[...], fourier_ref[...])
    total = height * channels
    for part in range(2):
        spectra_ref[part * total : (part + 1) * total, :] = found[:, part * orders : (part + 1) * orders]
    for row in range(height):
        real, imaginary = (
            spectra_ref[pl.ds(part * total + row, channels, stride=height), :] for part in range(2)
        )
        write_spectra(send_field_ref, row, real, imaginary)
    found = dot_nn(hidden_ref[...], fourier_ref[...])
    for row in range(inner):
        mine = found[row * channels : (row + 1) * channels, :]
        write_spectra(send_hidden_ref, row, mine[:, :orders], mine[:, orders:])


def rim_kernel(
    group, radius, rim_ref, edge_ref, before_ref, after_ref, fourier_ref,
    send_ref, partial_ref, hidden_ref,
):
    channels = edge_ref.shape[1]
    groups = channels // group
    orders = fourier_ref.shape[1] // 2
    rows = partial_ref.shape[0]
    depth = radius * group

    def per_group(g, carry):
        for side, halo_ref in enumerate((before_ref, after_ref)):
            rim = rim_ref[pl.ds(pl.multiple_of((g * 2 + side) * rows, 16), rows), :]
            halo = halo_ref[pl.ds(pl.multiple_of(g * depth, 16), depth), :]
            partial_ref[...] = dot_nn(rim, halo)
            for row in range(radius):
                total = shifted_sum(partial_ref, rows, depth, row * group, group)
                place = side * radius + row
                total = total + edge_ref[place, pl.ds(pl.multiple_of(g * group, 16), group), :]
                start = pl.multiple_of(place * channels + g * group, 16)
                hidden_ref[pl.ds(start, group), :] = gelu(total).astype(BF16)
        return carry

    lax.fori_loop(0, groups, per_group, 0)
    found = dot_nn(hidden_ref[...], fourier_ref[...])
    for row in range(2 * radius):
        mine = found[row * channels : (row + 1) * channels, :]
        write_spectra(send_ref, row, mine[:, :orders], mine[:, orders:])


def tables_kernel(group, turn_ref, sphere_ref, weight_ref, legendre_ref, mixing_ref, steps_ref, base_ref):
    taps = weight_ref.shape[0]
    radius = taps // 2
    channels = weight_ref.shape[3]
    owned, degrees, places = legendre_ref.shape
    wide = 2 * channels
    tiles = places // LANES
    first_order = lax.axis_index("lat") * owned + 1

    shape = (owned, places)
    order = (iota(shape, 0) + first_order).astype(F32)
    square = order * order
    cosine = jnp.broadcast_to(sphere_ref[0:1, :], shape)
    log_sine = jnp.broadcast_to(sphere_ref[1:2, :], shape)
    quadrature = jnp.broadcast_to(sphere_ref[2:3, :], shape)
    counts = (owned, ORDERS)
    number = (iota(counts, 1) + 1).astype(F32)
    ratio = jnp.where(
        iota(counts, 1) < iota(counts, 0) + first_order, jnp.log((2.0 * number - 1.0) / (2.0 * number)), 0.0
    )
    log_ratio = jnp.sum(ratio, axis=1, keepdims=True)
    diagonal = jnp.exp(0.5 * (jnp.log((2.0 * order + 1.0) / 2.0) + log_ratio) + order * log_sine)

    def advance(degree, carried):
        latest, before = carried
        real = jnp.full(shape, degree, jnp.int32).astype(F32)
        spread = jnp.maximum(real * real - square, 1.0)
        raising = jnp.sqrt(jnp.maximum(4.0 * real * real - 1.0, 1.0) / spread)
        previous = real - 1.0
        lowering = jnp.sqrt(
            jnp.maximum(previous * previous - square, 0.0) / jnp.maximum(4.0 * previous * previous - 1.0, 1.0)
        )
        raised = raising * (cosine * latest - lowering * before)
        result = jnp.where(real == order, diagonal, jnp.where(real > order, raised, 0.0))
        value = result * quadrature
        for tile in range(tiles):
            start = pl.multiple_of((tile * degrees + degree) * owned, owned)
            steps_ref[pl.ds(start, owned), :] = value[:, tile * LANES : (tile + 1) * LANES]
        return result, latest

    nothing = order * cosine * 0.0
    lax.fori_loop(0, degrees, advance, (nothing, nothing), unroll=8)
    half = degrees // 2
    for k in range(owned):
        for parity in range(2):
            for tile in range(tiles):
                start = tile * degrees * owned + parity * owned + k
                mine = steps_ref[pl.ds(start, half, stride=2 * owned), :]
                legendre_ref[
                    k, parity * half : (parity + 1) * half, tile * LANES : (tile + 1) * LANES
                ] = mine.astype(BF16)

    twice = (iota((channels, wide), 1) // 2 == iota((channels, wide), 0)).astype(F32).astype(BF16)
    across = (iota((group, wide), 1) % group == iota((group, wide), 0)).astype(F32).astype(BF16)
    shape = (wide, wide)
    row, column = iota(shape, 0), iota(shape, 1)
    row_part, column_part = row % 2, column // channels
    same_group = row // 2 // group == column % channels // group
    straight = row_part == column_part
    sign = jnp.where(row_part > column_part, 1.0, -1.0)

    def expanded(dy, dx):
        doubled = dot_nn(weight_ref[dy, dx], twice).astype(BF16)
        return dot_tn(doubled, across)

    for dy in range(taps):
        tap = [expanded(dy, dx) for dx in range(taps)]
        base_ref[dy, 0] = jnp.where(same_group & straight, tap[radius], 0.0)
        for far in range(1, radius + 1):
            high, low = tap[radius + far], tap[radius - far]
            both = jnp.where(straight, high + low, sign * (high - low))
            base_ref[dy, far] = jnp.where(same_group, both, 0.0)
    same_channel = straight & (row // 2 == column % channels)
    identity = same_channel.astype(F32).astype(BF16)

    def per_order(k, carry):
        factors = [
            jnp.where(straight, turn_ref[2 * far, k], turn_ref[2 * far + 1, k]) for far in range(radius)
        ]
        for dy in range(taps):
            total = base_ref[dy, 0]
            for far in range(radius):
                total = total + base_ref[dy, far + 1] * factors[far]
            mixing_ref[k, :, dy * wide : (dy + 1) * wide] = total.astype(BF16)
        mixing_ref[k, :, taps * wide :] = identity
        return carry

    lax.fori_loop(0, owned, per_order, 0)


def project_kernel(
    radius, field_ref, inner_ref, rim_ref, mixing_ref, legendre_ref, out_ref, rows_ref, plain_ref
):
    members, height, owned, wide = field_ref.shape
    places = members * height
    pad = radius * owned
    batch = out_ref.shape[0]
    step = pl.program_id(0)
    taps = 2 * radius + 1

    @pl.when(step == 0)
    def _():
        rows_ref[:pad, :] = jnp.zeros((pad, rows_ref.shape[1]), F32)
        rows_ref[pad + places * owned :, :] = jnp.zeros((pad, rows_ref.shape[1]), F32)
        for source in range(members):
            for row in range(height):
                start = (source * height + row) * owned
                plain_ref[start : start + owned, :wide] = field_ref[source, row].astype(F32)
                if radius <= row < height - radius:
                    mine = inner_ref[source, row - radius]
                else:
                    mine = rim_ref[source, row if row < radius else row - (height - 2 * radius)]
                rows_ref[pad + start : pad + start + owned, :wide] = mine.astype(F32)

    for at in range(batch):
        k = step * batch + at
        pieces = [rows_ref[pl.ds(dy * owned + k, places, stride=owned), :] for dy in range(taps)]
        pieces.append(plain_ref[pl.ds(k, places, stride=owned), :])
        stacked = jnp.concatenate([piece[:, :wide].astype(BF16) for piece in pieces], axis=1)
        mixed = dot_nt(mixing_ref[at], stacked).astype(BF16)
        found = dot_nt(mixed, legendre_ref[at][:, :places])
        half = found.shape[1] // 2
        out_ref[at, 0] = found[:, :half]
        out_ref[at, 1] = found[:, half:]


def per_device(atmosphere, first_weight, first_bias, second_weight):
    members = lax.axis_size("lat")
    position = lax.axis_index("lat")
    channels, height, length = atmosphere.shape
    group, taps = first_weight.shape[1], first_weight.shape[3]
    radius = taps // 2
    groups = channels // group
    inner = height - 2 * radius
    owned = ORDERS // members
    wide = 2 * channels
    places = height * members

    forward = [(i, i + 1) for i in range(members - 1)]
    backward = [(i + 1, i) for i in range(members - 1)]
    last = atmosphere[:, height - radius :].reshape(channels * radius, length)
    first = atmosphere[:, :radius].reshape(channels * radius, length)
    before = lax.ppermute(last, "lat", forward)
    after = lax.ppermute(first, "lat", backward)

    bias = jnp.broadcast_to(first_bias[:, None], (channels, 128))
    block = height * group
    rim_rows = taps * radius * group
    shapes = jax.ShapeDtypeStruct
    edge, rim, fourier, send_field, send_inner = call(
        lambda *refs: interior_kernel(group, *refs),
        "interior",
        (
            shapes((2 * radius, channels, length), F32),
            shapes((groups * 2 * rim_rows, radius * group), BF16),
            shapes((length, 2 * ORDERS), BF16),
            shapes((members, height, owned, wide), BF16),
            shapes((members, inner, owned, wide), BF16),
        ),
        [
            pltpu.VMEM((groups * taps * block, block), BF16),
            pltpu.VMEM((taps * block, length), F32),
            pltpu.VMEM((inner * channels, length), BF16),
            pltpu.VMEM((2 * height * channels, ORDERS), F32),
        ],
        2 * taps * block * block * length * groups,
        (first_weight.transpose(2, 3, 1, 0), bias, atmosphere.reshape(channels * height, length)),
    )
    got_field = lax.all_to_all(send_field, "lat", 0, 0, tiled=True)
    got_inner = lax.all_to_all(send_inner, "lat", 0, 0, tiled=True)

    send_rim = call(
        lambda *refs: rim_kernel(group, radius, *refs),
        "rim",
        shapes((members, 2 * radius, owned, wide), BF16),
        [
            pltpu.VMEM((rim_rows, length), F32),
            pltpu.VMEM((2 * radius * channels, length), BF16),
        ],
        2 * groups * 2 * rim_rows * radius * group * length,
        (rim, edge, before, after, fourier),
    )
    got_rim = lax.all_to_all(send_rim, "lat", 0, 0, tiled=True)

    angle = (position * owned + 1 + jnp.arange(owned, dtype=jnp.int32)).astype(F32) * (2.0 * math.pi / length)
    turns = jnp.stack([f(far * angle) for far in range(1, radius + 1) for f in (jnp.cos, jnp.sin)])
    colatitude = np.pi * (np.arange(places) + 0.5) / places
    cosine = np.cos(colatitude)
    cosine[places // 2 :] = -cosine[: places // 2][::-1]
    sine = np.sin(np.minimum(colatitude, colatitude[::-1]))
    sphere = np.stack([cosine, np.log(sine), np.pi * sine / np.sqrt(places)]).astype(np.float32)
    spread = -(-places // LANES) * LANES
    sphere = np.pad(sphere, ((0, 0), (0, spread - places)))
    lanes = max(wide, LANES)
    whole = pl.BlockSpec(memory_space=pltpu.VMEM)
    legendre, mixing = call(
        lambda *refs: tables_kernel(group, *refs),
        "tables",
        (
            shapes((owned, DEGREES, spread), BF16),
            shapes((owned, wide, (taps + 1) * wide), BF16),
        ),
        [
            pltpu.VMEM((spread // LANES * DEGREES * owned, LANES), F32),
            pltpu.VMEM((taps, radius + 1, wide, wide), F32),
        ],
        2 * owned * wide * taps * wide * 8,
        (turns, jnp.asarray(sphere), second_weight.transpose(2, 3, 1, 0)),
        in_specs=[pl.BlockSpec(memory_space=pltpu.SMEM), whole, whole],
    )

    batch = math.gcd(owned, 4)
    keep = lambda a: pl.BlockSpec(a.shape, lambda i: (0,) * a.ndim)
    cut = lambda a: pl.BlockSpec((batch,) + a.shape[1:], lambda i: (i,) + (0,) * (a.ndim - 1))
    out_shape = shapes((owned, 2, wide, DEGREES // 2), F32)
    spectrum = call(
        lambda *refs: project_kernel(radius, *refs),
        "project",
        out_shape,
        [
            pltpu.VMEM(((places + 2 * radius) * owned, lanes), F32),
            pltpu.VMEM((places * owned, lanes), F32),
        ],
        2 * owned * wide * places * ((taps + 1) * wide + DEGREES),
        (got_field, got_inner, got_rim, mixing, legendre),
        grid=(owned // batch,),
        in_specs=[keep(got_field), keep(got_inner), keep(got_rim), cut(mixing), cut(legendre)],
        out_specs=cut(out_shape),
    )
    return spectrum.reshape(owned, 2, channels, 2, DEGREES // 2)


def solution(mesh):
    placed = (
        P("chan", "lat", None),
        P("chan", None, None, None),
        P("chan"),
        P("chan", None, None, None),
    )
    return jax.shard_map(
        per_device,
        mesh=mesh,
        in_specs=placed,
        out_specs=P("lat", None, "chan", None, None),
        check_vma=False,
    )
```

time: 2890 us -> 62.6 us (0.02)
  matrix products: 2370 us -> 0 us
  local copies, waits for them, and re-layouts: 239 us -> 11.5 us
  loops' own time: 167 us -> 0 us
  other arithmetic: 47.2 us -> 0.11 us
    conv_general_dilated x2 -> x0, matrix products: 2370 us -> none  [convolve(): lax.conv_general_dilated(widened[None], kernel, (1, 1), 'VALID', feature_...]
    another operation x1 -> x0, loops' own time: 167 us -> none  [legendre(): lax.scan(advance, (empty_rows, empty_rows), jnp.arange(degrees, dtype=jnp...]
    broadcast_in_dim x4 -> x1, local copies, waits for them, and re-layouts: 141 us -> 0.07 us  [per_device(): bias = jnp.broadcast_to(first_bias[:, None], (channels, 128))]
    conv_general_dilated x2 -> x0, local copies, waits for them, and re-layouts: 60.8 us -> none  [convolve(): lax.conv_general_dilated(widened[None], kernel, (1, 1), 'VALID', feature_...]
  transfers between devices with their start and end apart: 9 -> 4, of which waited for: 5 -> 1; matrix products, arithmetic and copies ran while one was open for 2% -> 2% of each run, Pallas kernels for 0% -> 30%
where the time goes in v1:
time: 62.6 us; the launch traced here: 62 us
  Pallas kernels  24.8 us (40%)
  blocking collectives  12.3 us (20%)
  local copies, waits for them, and re-layouts  11.5 us (18%)
  starting transfers between devices  11.1 us (18%)
  waiting for transfers between devices  2.14 us (3%)
    pallas_call x4, Pallas kernels, call(): pl.pallas_call(kernel, out_shape=out_shape, in_specs=in_specs or [whole]...  24.8 us
    all_to_all x1, blocking collectives, per_device(): got_inner = lax.all_to_all(send_inner, 'lat', 0, 0, tiled=True)  12.3 us
    unnamed x20, local copies, waits for them, and re-layouts  7.08 us
    all_to_all x1, starting transfers between devices, per_device(): got_rim = lax.all_to_all(send_rim, 'lat', 0, 0, tiled=True)  4 us
    all_to_all x1, starting transfers between devices, per_device(): got_field = lax.all_to_all(send_field, 'lat', 0, 0, tiled=True)  3.41 us
    slice x1, local copies, waits for them, and re-layouts, per_device(): first = atmosphere[:, :radius].reshape(channels * radius, length)  2.51 us
    ppermute x1, starting transfers between devices, per_device(): before = lax.ppermute(last, 'lat', forward)  2.41 us
    all_to_all x1, waiting for transfers between devices, per_device(): got_field = lax.all_to_all(send_field, 'lat', 0, 0, tiled=True)  2.14 us
  transfers between devices with their start and end apart: 4, of which 1 were waited for; matrix products, arithmetic and copies ran while one was open for 2% of the time, Pallas kernels for 30%

profile of v1, /device:TPU:0, one launch (start us, length us, event | category | flops | bytes accessed | tf_op | source)
XLA Modules:
  0.0 62.0 jit_solution(1558251229147994695)
XLA Ops:
  0.0 0.0 copy-start.9
  0.0 2.5 %fusion.4 = (bf16[64,2,1536]{2,1,0:T(2,128)(2,1)S(1)}, bf16[64,2,1536]{2,1,0:T(2,128)(2,1)S(1)}) fusion(bf16[64,8,1536]{2,1,0:T(8,128)(2,1)} %param.5), kind=kLoop, calls=%fused_computation.8 | loop fusion | bytes 1572864 | tf_op jit(solution)/shard_map/slice | solution.py:355
  2.5 0.9 %reshape.45 = bf16[128,1536]{1,0:T(8,128)(2,1)} reshape(bf16[64,2,1536]{2,1,0:T(2,128)(2,1)S(1)} %get-tuple-element.20) | data formatting | bytes 786432 | tf_op jit(solution)/shard_map/reshape | solution.py:354
  3.4 2.4 %collective-permute-start = (bf16[128,1536]{1,0:T(8,128)(2,1)}, bf16[128,1536]{1,0:T(8,128)(2,1)S(1)}, u32[]{:S(2)}, u32[]{:S(2)}) collective-permute-start(bf16[128,1536]{1,0:T(8,128)(2,1)} %reshape.45), channel_id=1, source_target_pairs={{0,4},{4,8},{8,12},{12,16},{16,20},{20,24},{24,28},{1,5},{5,9},{9,... | collective-permute-start | bytes 1179656 | tf_op jit(solution)/shard_map/ppermute | solution.py:356
  5.8 0.9 %reshape.46 = bf16[128,1536]{1,0:T(8,128)(2,1)} reshape(bf16[64,2,1536]{2,1,0:T(2,128)(2,1)S(1)} %get-tuple-element.19) | data formatting | bytes 786432 | tf_op jit(solution)/shard_map/reshape | solution.py:355
  6.7 1.3 %collective-permute-start.1 = (bf16[128,1536]{1,0:T(8,128)(2,1)}, bf16[128,1536]{1,0:T(8,128)(2,1)S(1)}, u32[]{:S(2)}, u32[]{:S(2)}) collective-permute-start(bf16[128,1536]{1,0:T(8,128)(2,1)} %reshape.46), channel_id=1, source_target_pairs={{4,0},{8,4},{12,8},{16,12},{20,16},{24,20},{28,24},{5,1},{9,5},{13... | collective-permute-start | bytes 1179656 | tf_op jit(solution)/shard_map/ppermute | solution.py:357
  8.0 0.0 copy-done.9
  8.0 0.1 broadcast_in_dim.2.refs_1_
  8.1 0.0 copy-start.2
  8.1 1.4 %copy-done.2 = bf16[64,8,1536]{2,1,0:T(8,128)(2,1)S(1)} copy-done((bf16[64,8,1536]{2,1,0:T(8,128)(2,1)S(1)}, bf16[64,8,1536]{2,1,0:T(8,128)(2,1)}, u32[]{:S(2)}) %copy-start.2) | copy-done | bytes 1572888
  9.5 0.0 copy-start.8
  9.5 0.9 %copy-done.8 = bf16[64,16,5,5]{0,1,3,2:T(8,128)(2,1)S(1)} copy-done((bf16[64,16,5,5]{0,1,3,2:T(8,128)(2,1)S(1)}, bf16[64,16,5,5]{0,1,3,2:T(8,128)(2,1)}, u32[]{:S(2)}) %copy-start.8) | copy-done | bytes 51224
  10.4 6.2 %interior.1 = (f32[4,64,1536]{2,1,0:T(8,128)S(1)}, bf16[1280,32]{1,0:T(8,128)(2,1)S(1)}, bf16[1536,256]{1,0:T(8,128)(2,1)S(1)}, bf16[8,8,16,128]{3,2,1,0:T(8,128)(2,1)S(1)}, bf16[8,4,16,128]{3,2,1,0:T(8,128)(2,1)S(1)}) custom-call(bf16[5,5,16,64]{3,2,1,0:T(8,128)(2,1)S(1)} %bitcast.6, f32[64,128]{1,0:T(8,128)S(1)} %broadcast_in_dim.2.refs_1_, ...), custom_call_target="tpu_custom_call" | custom-call | flops 1006632960 | bytes 4491264 | tf_op jit(solution)/shard_map/interior/pallas_call | solution.py:43
  16.6 0.0 copy-start.3
  16.6 0.7 %copy-done.3 = bf16[1280,32]{1,0:T(8,128)(2,1)} copy-done((bf16[1280,32]{1,0:T(8,128)(2,1)}, bf16[1280,32]{1,0:T(8,128)(2,1)S(1)}, u32[]{:S(2)}) %copy-start.3) | copy-done | bytes 81944
  17.4 0.0 copy-start.5
  17.4 12.3 %all_to_all.15.refs_1_ = bf16[8,4,16,128]{3,2,1,0:T(8,128)(2,1)S(1)} all-to-all(bf16[8,4,16,128]{3,2,1,0:T(8,128)(2,1)S(1)} %get-tuple-element.13), channel_id=1, replica_groups=mesh['lat'=8,'chan'=4] {'lat'}, dimensions={0} | all-to-all | bytes 262144 | tf_op jit(solution)/shard_map/all_to_all | solution.py:383
  29.7 0.0 copy-done.5
  29.7 3.4 %all-to-all-start = ((bf16[8,8,16,128]{3,2,1,0:T(8,128)(2,1)}), bf16[8,8,16,128]{3,2,1,0:T(8,128)(2,1)S(1)}, u32[]{:S(2)}, u32[]{:S(2)}) async-start(bf16[8,8,16,128]{3,2,1,0:T(8,128)(2,1)} %copy-done.5), calls=%async_computation | async-start | bytes 524288 | tf_op jit(solution)/shard_map/all_to_all | solution.py:382
  33.2 0.0 collective-permute-done.refs_2_
  33.2 0.0 collective-permute-done.1.refs_3_
  33.2 0.0 copy-start.4
  33.2 1.0 %copy-done.4 = bf16[1280,32]{1,0:T(8,128)(2,1)S(1)} copy-done((bf16[1280,32]{1,0:T(8,128)(2,1)S(1)}, bf16[1280,32]{1,0:T(8,128)(2,1)}, u32[]{:S(2)}) %copy-start.4) | copy-done | bytes 81944
  34.2 0.0 copy-start.7
  34.2 3.7 %rim.1 = bf16[8,4,16,128]{3,2,1,0:T(8,128)(2,1)} custom-call(bf16[1280,32]{1,0:T(8,128)(2,1)S(1)} %copy-done.4, f32[4,64,1536]{2,1,0:T(8,128)S(1)} %get-tuple-element.15.refs_1_, bf16[128,1536]{1,0:T(8,128)(2,1)S(1)} %collective-permute-done.refs_2_, bf16[128,1536]{1,0:T(8,128)(2,1)S(1)} %collective-permute-done.1.refs_3_, ...), custom_call_target="tpu_custom_call" | custom-call | flops 125829120 | bytes 3358720 | tf_op jit(solution)/shard_map/rim/pallas_call | solution.py:43
  37.8 2.1 %all-to-all-done.refs_0_ = bf16[8,8,16,128]{3,2,1,0:T(8,128)(2,1)S(1)} async-done(((bf16[8,8,16,128]{3,2,1,0:T(8,128)(2,1)}), bf16[8,8,16,128]{3,2,1,0:T(8,128)(2,1)S(1)}, u32[]{:S(2)}, u32[]{:S(2)}) %all-to-all-start) | async-done | bytes 262176 | tf_op jit(solution)/shard_map/all_to_all | solution.py:382
  40.0 4.0 %all-to-all-start.2 = ((bf16[8,4,16,128]{3,2,1,0:T(8,128)(2,1)}), bf16[8,4,16,128]{3,2,1,0:T(8,128)(2,1)}, u32[]{:S(2)}, u32[]{:S(2)}) async-start(bf16[8,4,16,128]{3,2,1,0:T(8,128)(2,1)} %rim.1), calls=%async_computation.2 | async-start | bytes 262144 | tf_op jit(solution)/shard_map/all_to_all | solution.py:396
  44.0 0.0 copy-done.7
  44.0 0.0 copy-start.6
  44.1 0.9 %copy-done.6 = bf16[64,16,5,5]{0,1,3,2:T(8,128)(2,1)S(1)} copy-done((bf16[64,16,5,5]{0,1,3,2:T(8,128)(2,1)S(1)}, bf16[64,16,5,5]{0,1,3,2:T(8,128)(2,1)}, u32[]{:S(2)}) %copy-start.6) | copy-done | bytes 51224
  44.9 8.8 %tables.1 = (bf16[16,256,128]{2,1,0:T(8,128)(2,1)S(1)}, bf16[16,128,768]{2,1,0:T(8,128)(2,1)S(1)}) custom-call(f32[4,16]{1,0:T(4,128)S(1)} %pad_maximum_fusion.refs_0_, f32[3,128]{1,0:T(4,128)S(1)} %copy-done.7, bf16[5,5,16,64]{3,2,1,0:T(8,128)(2,1)S(1)} %bitcast.5), custom_call_target="tpu_custom_call" | custom-call | flops 20971520 | bytes 4247296 | tf_op jit(solution)/shard_map/tables/pallas_call | solution.py:43
  53.7 0.0 copy-start
  53.7 1.0 %copy-done = bf16[16,256,128]{2,1,0:T(8,128)(2,1)} copy-done((bf16[16,256,128]{2,1,0:T(8,128)(2,1)}, bf16[16,256,128]{2,1,0:T(8,128)(2,1)S(1)}, u32[]{:S(2)}) %copy-start) | copy-done | bytes 1048600
  54.7 0.0 all-to-all-done.2.refs_2_
  54.7 0.0 copy-start.1
  54.7 1.2 %copy-done.1 = bf16[16,256,128]{2,1,0:T(8,128)(2,1)S(1)} copy-done((bf16[16,256,128]{2,1,0:T(8,128)(2,1)S(1)}, bf16[16,256,128]{2,1,0:T(8,128)(2,1)}, u32[]{:S(2)}) %copy-start.1) | copy-done | bytes 1048600
  55.9 6.1 %project.1 = f32[16,2,128,128]{3,2,1,0:T(8,128)} custom-call(bf16[8,8,16,128]{3,2,1,0:T(8,128)(2,1)S(1)} %all-to-all-done.refs_0_, bf16[8,4,16,128]{3,2,1,0:T(8,128)(2,1)S(1)} %all_to_all.15.refs_1_, bf16[8,4,16,128]{3,2,1,0:T(8,128)(2,1)} %all-to-all-done.2.refs_2_, bf16[16,128,768]{2,1,0:T(8,128)(2,1)S(1)} %get-tuple-element.17.refs_3_, ...), custom_call_target="tpu_custom_call" | custom-call | flops 268435456 | bytes 6815744 | tf_op jit(solution)/shard_map/project/pallas_call | solution.py:43
  (3 shorter events, 0.1 us)
Async XLA Ops:
  0.0 8.0 %copy-start.9 = (f32[64]{0:T(128)S(1)}, f32[64]{0:T(128)}, u32[]{:S(2)}) copy-start(f32[64]{0:T(128)} %param.7) | copy-start | bytes 772
  3.4 29.8 %collective-permute-start = (bf16[128,1536]{1,0:T(8,128)(2,1)}, bf16[128,1536]{1,0:T(8,128)(2,1)S(1)}, u32[]{:S(2)}, u32[]{:S(2)}) collective-permute-start(bf16[128,1536]{1,0:T(8,128)(2,1)} %reshape.45), channel_id=1, source_target_pairs={{0,4},{4,8},{8,12},{12,16},{16,20},{20,24},{24,28},{1,5},{5,9},{9,... | collective-permute-start | bytes 1179656 | tf_op jit(solution)/shard_map/ppermute | solution.py:356
  6.7 26.5 %collective-permute-start.1 = (bf16[128,1536]{1,0:T(8,128)(2,1)}, bf16[128,1536]{1,0:T(8,128)(2,1)S(1)}, u32[]{:S(2)}, u32[]{:S(2)}) collective-permute-start(bf16[128,1536]{1,0:T(8,128)(2,1)} %reshape.46), channel_id=1, source_target_pairs={{4,0},{8,4},{12,8},{16,12},{20,16},{24,20},{28,24},{5,1},{9,5},{13... | collective-permute-start | bytes 1179656 | tf_op jit(solution)/shard_map/ppermute | solution.py:357
  8.1 1.4 %copy-start.2 = (bf16[64,8,1536]{2,1,0:T(8,128)(2,1)S(1)}, bf16[64,8,1536]{2,1,0:T(8,128)(2,1)}, u32[]{:S(2)}) copy-start(bf16[64,8,1536]{2,1,0:T(8,128)(2,1)} %param.5) | copy-start | bytes 4718596
  9.5 0.9 %copy-start.8 = (bf16[64,16,5,5]{0,1,3,2:T(8,128)(2,1)S(1)}, bf16[64,16,5,5]{0,1,3,2:T(8,128)(2,1)}, u32[]{:S(2)}) copy-start(bf16[64,16,5,5]{0,1,3,2:T(8,128)(2,1)} %param.6) | copy-start | bytes 153604
  16.6 0.7 %copy-start.3 = (bf16[1280,32]{1,0:T(8,128)(2,1)}, bf16[1280,32]{1,0:T(8,128)(2,1)S(1)}, u32[]{:S(2)}) copy-start(bf16[1280,32]{1,0:T(8,128)(2,1)S(1)} %get-tuple-element.14.refs_0_) | copy-start | bytes 245764
  17.4 12.3 %copy-start.5 = (bf16[8,8,16,128]{3,2,1,0:T(8,128)(2,1)}, bf16[8,8,16,128]{3,2,1,0:T(8,128)(2,1)S(1)}, u32[]{:S(2)}) copy-start(bf16[8,8,16,128]{3,2,1,0:T(8,128)(2,1)S(1)} %get-tuple-element.12) | copy-start | bytes 786436
  29.7 10.3 %all-to-all-start = ((bf16[8,8,16,128]{3,2,1,0:T(8,128)(2,1)}), bf16[8,8,16,128]{3,2,1,0:T(8,128)(2,1)S(1)}, u32[]{:S(2)}, u32[]{:S(2)}) async-start(bf16[8,8,16,128]{3,2,1,0:T(8,128)(2,1)} %copy-done.5), calls=%async_computation | async-start | bytes 524288 | tf_op jit(solution)/shard_map/all_to_all | solution.py:382
  33.2 1.0 %copy-start.4 = (bf16[1280,32]{1,0:T(8,128)(2,1)S(1)}, bf16[1280,32]{1,0:T(8,128)(2,1)}, u32[]{:S(2)}) copy-start(bf16[1280,32]{1,0:T(8,128)(2,1)} %copy-done.3) | copy-start | bytes 245764
  34.2 9.9 %copy-start.7 = (f32[3,128]{1,0:T(4,128)S(1)}, f32[3,128]{1,0:T(4,128)}, u32[]{:S(2)}) copy-start(f32[3,128]{1,0:T(4,128)} %constant.17.clone.refs_1_) | copy-start | bytes 4612
  40.0 14.7 %all-to-all-start.2 = ((bf16[8,4,16,128]{3,2,1,0:T(8,128)(2,1)}), bf16[8,4,16,128]{3,2,1,0:T(8,128)(2,1)}, u32[]{:S(2)}, u32[]{:S(2)}) async-start(bf16[8,4,16,128]{3,2,1,0:T(8,128)(2,1)} %rim.1), calls=%async_computation.2 | async-start | bytes 262144 | tf_op jit(solution)/shard_map/all_to_all | solution.py:396
  44.0 0.9 %copy-start.6 = (bf16[64,16,5,5]{0,1,3,2:T(8,128)(2,1)S(1)}, bf16[64,16,5,5]{0,1,3,2:T(8,128)(2,1)}, u32[]{:S(2)}) copy-start(bf16[64,16,5,5]{0,1,3,2:T(8,128)(2,1)} %param.8) | copy-start | bytes 153604
  53.7 1.0 %copy-start = (bf16[16,256,128]{2,1,0:T(8,128)(2,1)}, bf16[16,256,128]{2,1,0:T(8,128)(2,1)S(1)}, u32[]{:S(2)}) copy-start(bf16[16,256,128]{2,1,0:T(8,128)(2,1)S(1)} %get-tuple-element.18.refs_4_) | copy-start | bytes 3145732
  54.7 1.2 %copy-start.1 = (bf16[16,256,128]{2,1,0:T(8,128)(2,1)S(1)}, bf16[16,256,128]{2,1,0:T(8,128)(2,1)}, u32[]{:S(2)}) copy-start(bf16[16,256,128]{2,1,0:T(8,128)(2,1)} %copy-done) | copy-start | bytes 3145732

commit v2 on v1

v2 whole, which is shorter than its diff:
```python
import math

import jax
import jax.numpy as jnp
import numpy as np
from jax import lax
from jax.experimental import pallas as pl
from jax.experimental.pallas import tpu as pltpu
from jax.sharding import PartitionSpec as P

ORDERS = 128
DEGREES = 256
LANES = 128
F32 = jnp.float32
BF16 = jnp.bfloat16


def dot_tn(left, right):
    return lax.dot_general(left, right, (((0,), (0,)), ((), ())), preferred_element_type=F32)


def dot_nt(left, right):
    return lax.dot_general(left, right, (((1,), (1,)), ((), ())), preferred_element_type=F32)


def dot_nn(left, right):
    return jnp.dot(left, right, preferred_element_type=F32)


def iota(shape, dim):
    return lax.broadcasted_iota(jnp.int32, shape, dim)


def gelu(value):
    return 0.5 * value * (1.0 + lax.erf(value * math.sqrt(0.5)))


VMEM = pl.BlockSpec(memory_space=pltpu.VMEM)
SMEM = pl.BlockSpec(memory_space=pltpu.SMEM)
HBM = pl.BlockSpec(memory_space=pltpu.HBM)


def bytes_of(arrays):
    return sum(math.prod(a.shape) * a.dtype.itemsize for a in jax.tree.leaves(arrays))


def call(kernel, name, out_shape, scratch, mebibytes, flops, args, in_specs=None, out_specs=None):
    size = bytes_of((args, out_shape))
    return pl.pallas_call(
        kernel,
        out_shape=out_shape,
        in_specs=in_specs or [VMEM] * len(args),
        out_specs=out_specs or jax.tree.map(lambda _: VMEM, out_shape),
        scratch_shapes=scratch,
        compiler_params=pltpu.CompilerParams(vmem_limit_bytes=mebibytes * 2**20),
        cost_estimate=pl.CostEstimate(flops=flops, transcendentals=0, bytes_accessed=size),
        name=name,
    )(*args)


def turned(number, length):
    number = number.astype(F32)
    number = number - length * jnp.floor(number / length)
    return number * (2.0 * math.pi / length)


def write_fourier(fourier_ref, length, orders):
    tile = 128
    factor = 1.0 / math.sqrt(length)
    shape = (tile, orders)
    fine = turned(iota(shape, 0) * (iota(shape, 1) + 1), length)
    fine_cos, fine_sin = jnp.cos(fine), jnp.sin(fine)
    blocks = length // tile
    padded = -(-blocks // 8) * 8
    shape = (padded, orders)
    coarse = turned(iota(shape, 0) * tile * (iota(shape, 1) + 1), length)
    coarse_cos, coarse_sin = jnp.cos(coarse) * factor, jnp.sin(coarse) * factor
    for block in range(blocks):
        cosine = coarse_cos[block : block + 1, :]
        sine = coarse_sin[block : block + 1, :]
        rows = slice(block * tile, (block + 1) * tile)
        fourier_ref[rows, :orders] = (cosine * fine_cos - sine * fine_sin).astype(BF16)
        fourier_ref[rows, orders:] = (-(sine * fine_cos + cosine * fine_sin)).astype(BF16)


def write_spectra(send_ref, slot, real, imaginary):
    members, _, owned, _ = send_ref.shape
    flipped = jnp.concatenate([real, imaginary], axis=0).T
    for device in range(members):
        send_ref[device, slot] = flipped[device * owned : (device + 1) * owned, :].astype(BF16)


def taps_of(weight_ref, dx):
    return jnp.concatenate([weight_ref[dy, dx] for dy in range(weight_ref.shape[0])], axis=0)


def shifted_sum(partial_ref, rows, height, first, count):
    taps = rows // height
    radius = taps // 2
    total = None
    for dx in range(taps):
        start = dx * height + first
        piece = partial_ref[start : start + count, :]
        if dx != radius:
            piece = pltpu.roll(piece, (radius - dx) % piece.shape[1], 1)
        total = piece if total is None else total + piece
    return total


def edges_kernel(group, radius, groups, field_ref, pair_ref, cross_ref):
    block = field_ref.shape[0] // groups
    height = block // group
    depth = radius * group
    parity = lax.axis_index("lat") % 2
    shape = (2 * depth, block)
    place, column = iota(shape, 0), iota(shape, 1)
    far = (place // depth + parity) % 2 == 0
    row = place % radius + jnp.where(far, height - radius, 0)
    chosen = column == place % depth // radius * height + row
    selector = chosen.astype(F32).astype(BF16)
    for g in range(groups):
        found = dot_nn(selector, field_ref[g * block : (g + 1) * block, :]).astype(BF16)
        pair_ref[g * depth : (g + 1) * depth, :] = found[:depth, :]
        cross_ref[g * depth : (g + 1) * depth, :] = found[depth:, :]


def interior_kernel(
    group, weight_ref, bias_ref, field_ref,
    edge_ref, rim_ref, fourier_ref, send_ref,
    band_ref, partial_ref, hidden_ref, spectra_ref,
):
    taps = weight_ref.shape[0]
    radius = taps // 2
    channels = weight_ref.shape[3]
    groups = channels // group
    height = field_ref.shape[0] // channels
    orders = fourier_ref.shape[1] // 2
    inner = height - 2 * radius
    block = height * group
    rows = taps * block

    write_fourier(fourier_ref, field_ref.shape[1], orders)
    shape = (taps * group, height * block)
    place = iota(shape, 0)
    column = iota(shape, 1)
    out_row, column = column // block, column % block
    chosen = (place % group == column // height) & (place // group == column % height - out_row + radius)
    selector = chosen.astype(F32).astype(BF16)
    rim_shape = (taps * group, radius * group)
    rim_place = iota(rim_shape, 0)
    rim_column = iota(rim_shape, 1)
    same = rim_place % group == rim_column // radius
    rim_row = rim_column % radius
    rim_rows = taps * radius * group
    for dx in range(taps):
        mine = taps_of(weight_ref, dx)
        spread = dot_tn(mine, selector).astype(BF16)
        for g in range(groups):
            for row in range(height):
                start = g * rows + dx * block + row * group
                band_ref[start : start + group, :] = spread[
                    g * group : (g + 1) * group, row * block : (row + 1) * block
                ]
        for side in range(2):
            for row in range(radius):
                tap = rim_row - row + (0 if side == 0 else taps - 1)
                pick = (same & (rim_place // group == tap)).astype(F32).astype(BF16)
                spread = dot_tn(mine, pick).astype(BF16)
                for g in range(groups):
                    start = (g * 2 + side) * rim_rows + (dx * radius + row) * group
                    rim_ref[start : start + group, :] = spread[g * group : (g + 1) * group, :]

    def per_group(g, carry):
        band = band_ref[pl.ds(pl.multiple_of(g * rows, 16), rows), :]
        field = field_ref[pl.ds(pl.multiple_of(g * block, 16), block), :]
        partial_ref[...] = dot_nn(band, field)
        mine = pl.ds(pl.multiple_of(g * group, 16), group)
        bias = bias_ref[mine, :][:, :1]
        for row in range(height):
            total = shifted_sum(partial_ref, rows, block, row * group, group) + bias
            if radius <= row < height - radius:
                start = pl.multiple_of((row - radius) * channels + g * group, 16)
                hidden_ref[pl.ds(start, group), :] = gelu(total).astype(BF16)
            else:
                edge_ref[row if row < radius else row - inner, mine, :] = total
        return carry

    lax.fori_loop(0, groups, per_group, 0)

    found = dot_nn(field_ref[...], fourier_ref[...])
    total = height * channels
    for part in range(2):
        spectra_ref[part * total : (part + 1) * total, :] = found[:, part * orders : (part + 1) * orders]
    for row in range(height):
        real, imaginary = (
            spectra_ref[pl.ds(part * total + row, channels, stride=height), :] for part in range(2)
        )
        write_spectra(send_ref, row, real, imaginary)
    found = dot_nn(hidden_ref[...], fourier_ref[...])
    for row in range(inner):
        mine = found[row * channels : (row + 1) * channels, :]
        write_spectra(send_ref, height + row, mine[:, :orders], mine[:, orders:])


def rim_kernel(
    group, radius, rim_ref, edge_ref, pair_ref, cross_ref, fourier_ref, early_ref,
    send_ref, partial_ref, hidden_ref,
):
    channels = edge_ref.shape[1]
    groups = channels // group
    orders = fourier_ref.shape[1] // 2
    rows = partial_ref.shape[0]
    depth = radius * group
    early = early_ref.shape[1]
    position = lax.axis_index("lat")
    parity = position % 2
    polar = (position == 0) | (position == lax.axis_size("lat") - 1)

    def per_group(g, carry):
        for halo_ref, side in ((pair_ref, 1 - parity), (cross_ref, parity)):
            rim = rim_ref[pl.ds(pl.multiple_of((g * 2 + side) * rows, 16), rows), :]
            if halo_ref is cross_ref:
                rim = jnp.where(polar, jnp.zeros_like(rim), rim)
            halo = halo_ref[pl.ds(pl.multiple_of(g * depth, 16), depth), :]
            partial_ref[...] = dot_nn(rim, halo)
            for row in range(radius):
                total = shifted_sum(partial_ref, rows, depth, row * group, group)
                place = side * radius + row
                total = total + edge_ref[place, pl.ds(pl.multiple_of(g * group, 16), group), :]
                start = pl.multiple_of(place * channels + g * group, 16)
                hidden_ref[pl.ds(start, group), :] = gelu(total).astype(BF16)
        return carry

    lax.fori_loop(0, groups, per_group, 0)
    send_ref[:, :early] = early_ref[...]
    found = dot_nn(hidden_ref[...], fourier_ref[...])
    for row in range(2 * radius):
        mine = found[row * channels : (row + 1) * channels, :]
        write_spectra(send_ref, early + row, mine[:, :orders], mine[:, orders:])


def tables_kernel(
    group, turn_ref, sphere_ref, weight_ref,
    table_ref,
    steps_ref, rate_ref, base_ref, turned_ref,
):
    taps = weight_ref.shape[0]
    radius = taps // 2
    channels = weight_ref.shape[3]
    degrees = rate_ref.shape[0] // 2
    owned = table_ref.shape[0]
    wide = 2 * channels
    head = sphere_ref.shape[1]
    places = head * LANES // owned
    first_order = lax.axis_index("lat") * owned + 1

    shape = (degrees, LANES)
    order = (iota(shape, 1) % owned + first_order).astype(F32)
    degree = iota(shape, 0).astype(F32)
    previous = degree - 1.0
    raising = jnp.sqrt(
        jnp.maximum(4.0 * degree * degree - 1.0, 1.0) / jnp.maximum(degree * degree - order * order, 1.0)
    )
    lowering = jnp.sqrt(
        jnp.maximum(previous * previous - order * order, 0.0)
        / jnp.maximum(4.0 * previous * previous - 1.0, 1.0)
    )
    rate_ref[:degrees, :] = raising
    rate_ref[degrees:, :] = lowering

    shape = (ORDERS, LANES)
    number = (iota(shape, 0) + 1).astype(F32)
    ratio = jnp.where(
        iota(shape, 0) < iota(shape, 1) % owned + first_order, jnp.log((2.0 * number - 1.0) / (2.0 * number)), 0.0
    )
    log_ratio = jnp.sum(ratio, axis=0, keepdims=True)
    shape = (head, LANES)
    whole_order = iota(shape, 1) % owned + first_order
    order = whole_order.astype(F32)
    cosine, log_sine, quadrature = sphere_ref[0], sphere_ref[1], sphere_ref[2]
    diagonal = jnp.exp(0.5 * (jnp.log((2.0 * order + 1.0) / 2.0) + log_ratio) + order * log_sine)

    twice = (iota((channels, wide), 1) // 2 == iota((channels, wide), 0)).astype(F32).astype(BF16)
    across = (iota((group, wide), 1) % group == iota((group, wide), 0)).astype(F32).astype(BF16)
    shape = (wide, wide)
    row, column = iota(shape, 0), iota(shape, 1)
    row_part, column_part = row % 2, column // channels
    same_group = row // 2 // group == column % channels // group
    straight = row_part == column_part
    sign = jnp.where(row_part > column_part, 1.0, -1.0)
    flat = jnp.concatenate([weight_ref[dy, dx] for dy in range(taps) for dx in range(taps)], axis=0)
    doubled = dot_nn(flat, twice).astype(BF16)

    def expanded(dy, dx):
        start = (dy * taps + dx) * group
        return dot_tn(doubled[start : start + group, :], across)

    for dy in range(taps):
        tap = [expanded(dy, dx) for dx in range(taps)]
        base_ref[dy, 0] = jnp.where(same_group & straight, tap[radius], 0.0)
        for far in range(1, radius + 1):
            high, low = tap[radius + far], tap[radius - far]
            both = jnp.where(straight, high + low, sign * (high - low))
            base_ref[dy, far] = jnp.where(same_group, both, 0.0)
    steps = degrees // owned

    def per_order(k, carried):
        latest, before = carried
        for step in range(steps):
            at = k * steps + step
            up = jnp.broadcast_to(rate_ref[pl.ds(at, 1), :], (head, LANES))
            down = jnp.broadcast_to(rate_ref[pl.ds(degrees + at, 1), :], (head, LANES))
            raised = up * (cosine * latest - down * before)
            latest, before = jnp.where(whole_order == at, diagonal, raised), latest
            steps_ref[pl.ds(pl.multiple_of(at * head, 8), head), :] = latest * quadrature
        factors = [
            jnp.where(straight, turn_ref[2 * far, k], turn_ref[2 * far + 1, k]) for far in range(radius)
        ]
        for dy in range(taps):
            total = base_ref[dy, 0]
            for far in range(radius):
                total = total + base_ref[dy, far + 1] * factors[far]
            table_ref[k, :wide, dy * wide : (dy + 1) * wide] = total.astype(BF16)
        return latest, before

    nothing = order * cosine * 0.0
    lax.fori_loop(0, owned, per_order, (nothing, nothing))
    half = degrees // 2
    total = head * LANES
    for parity in range(2):
        for at in range(head):
            mine = steps_ref[pl.ds(parity * head + at, half, stride=2 * head), :]
            turned_ref[parity * total + at * LANES : parity * total + (at + 1) * LANES, :] = mine.T
    for parity in range(2):
        for k in range(owned):
            mine = turned_ref[pl.ds(parity * total + k, places, stride=owned), :]
            rows = slice(parity * places, (parity + 1) * places)
            table_ref[k, rows, taps * wide :] = mine.astype(BF16)


def project_kernel(
    radius, got_ref, table_ref, out_hbm, rows_ref, plain_ref, out_ref, semaphores
):
    members, height, owned, wide = got_ref.shape
    height = height // 2
    places = members * height
    pad = radius * owned
    taps = 2 * radius + 1
    slots = out_ref.shape[0]

    rows_ref[:pad, :] = jnp.zeros((pad, rows_ref.shape[1]), F32)
    rows_ref[pad + places * owned :, :] = jnp.zeros((pad, rows_ref.shape[1]), F32)
    for source in range(members):
        for row in range(height):
            start = (source * height + row) * owned
            plain_ref[start : start + owned, :wide] = got_ref[source, row].astype(F32)
            if radius <= row < height - radius:
                place = height + row - radius
            elif row < radius:
                place = 2 * height - 2 * radius + row
            else:
                place = height + row
            rows_ref[pad + start : pad + start + owned, :wide] = got_ref[source, place].astype(F32)

    row, column = iota((wide, wide), 0), iota((wide, wide), 1)
    identity = (column == row % 2 * (wide // 2) + row // 2).astype(F32).astype(BF16)

    def sent(k, slot):
        return pltpu.make_async_copy(out_ref.at[slot], out_hbm.at[k], semaphores.at[slot])

    for k in range(owned):
        slot = k % slots
        pieces = [rows_ref[pl.ds(dy * owned + k, places, stride=owned), :] for dy in range(taps)]
        pieces.append(plain_ref[pl.ds(k, places, stride=owned), :])
        stacked = jnp.concatenate([piece[:, :wide].astype(BF16) for piece in pieces], axis=1)
        mixing = jnp.concatenate([table_ref[k, :wide, : taps * wide], identity], axis=1)
        mixed = dot_nt(mixing, stacked).astype(BF16)
        if k >= slots:
            sent(k - slots, slot).wait()
        for parity in range(2):
            rows = slice(parity * places, (parity + 1) * places)
            out_ref[slot, parity] = dot_nn(mixed, table_ref[k, rows, taps * wide :])
        sent(k, slot).start()
    for k in range(max(0, owned - slots), owned):
        sent(k, k % slots).wait()


def per_device(atmosphere, first_weight, first_bias, second_weight):
    members = lax.axis_size("lat")
    position = lax.axis_index("lat")
    channels, height, length = atmosphere.shape
    group, taps = first_weight.shape[1], first_weight.shape[3]
    radius = taps // 2
    groups = channels // group
    inner = height - 2 * radius
    owned = ORDERS // members
    wide = 2 * channels
    places = height * members

    shapes = jax.ShapeDtypeStruct
    block = height * group
    rim_rows = taps * radius * group
    first_taps = first_weight.transpose(2, 3, 1, 0)
    second_taps = second_weight.transpose(2, 3, 1, 0)
    flat = atmosphere.reshape(channels * height, length)
    pair, cross = call(
        lambda *refs: edges_kernel(group, radius, groups, *refs),
        "edges",
        (shapes((channels * radius, length), BF16), shapes((channels * radius, length), BF16)),
        [],
        8,
        4 * radius * channels * block * length,
        (flat,),
    )
    pairs = [(i, i ^ 1) for i in range(members) if i ^ 1 < members]
    crosses = [(i, (i + 1 if i % 2 else i - 1) % members) for i in range(members)]
    cross = lax.ppermute(cross, "lat", crosses)
    pair = lax.ppermute(pair, "lat", pairs)

    bias = jnp.broadcast_to(first_bias[:, None], (channels, LANES))
    edge, rim, fourier, early = call(
        lambda *refs: interior_kernel(group, *refs),
        "interior",
        (
            shapes((2 * radius, channels, length), F32),
            shapes((groups * 2 * rim_rows, radius * group), BF16),
            shapes((length, 2 * ORDERS), BF16),
            shapes((members, height + inner, owned, wide), BF16),
        ),
        [
            pltpu.VMEM((groups * taps * block, block), BF16),
            pltpu.VMEM((taps * block, length), F32),
            pltpu.VMEM((inner * channels, length), BF16),
            pltpu.VMEM((2 * height * channels, ORDERS), F32),
        ],
        10,
        2 * taps * block * block * length * groups,
        (first_taps, bias, flat),
    )
    send = call(
        lambda *refs: rim_kernel(group, radius, *refs),
        "rim",
        shapes((members, 2 * height, owned, wide), BF16),
        [
            pltpu.VMEM((rim_rows, length), F32),
            pltpu.VMEM((2 * radius * channels, length), BF16),
        ],
        6,
        2 * groups * 2 * rim_rows * radius * group * length,
        (rim, edge, pair, cross, fourier, early),
    )
    got = lax.all_to_all(send, "lat", 0, 0, tiled=True)

    angle = (position * owned + 1 + jnp.arange(owned, dtype=jnp.int32)).astype(F32) * (2.0 * math.pi / length)
    turns = jnp.stack([f(far * angle) for far in range(1, radius + 1) for f in (jnp.cos, jnp.sin)])
    colatitude = np.pi * (np.arange(places) + 0.5) / places
    cosine = np.cos(colatitude)
    cosine[places // 2 :] = -cosine[: places // 2][::-1]
    sine = np.sin(np.minimum(colatitude, colatitude[::-1]))
    sphere = np.stack([cosine, np.log(sine), np.pi * sine / np.sqrt(places)]).astype(np.float32)
    head = places * owned // LANES
    sphere = np.repeat(sphere.reshape(3, head, LANES // owned), owned, axis=2)
    table = call(
        lambda *refs: tables_kernel(group, *refs),
        "tables",
        shapes((owned, max(wide, 2 * places), taps * wide + DEGREES // 2), BF16),
        [
            pltpu.VMEM((DEGREES * head, LANES), F32),
            pltpu.VMEM((2 * DEGREES, LANES), F32),
            pltpu.VMEM((taps, radius + 1, wide, wide), F32),
            pltpu.VMEM((2 * head * LANES, DEGREES // 2), F32),
        ],
        6,
        2 * owned * wide * taps * wide * 8,
        (turns, jnp.asarray(sphere), second_taps),
        in_specs=[SMEM, VMEM, VMEM],
    )

    lanes = max(wide, LANES)
    slots = owned
    spectrum = call(
        lambda *refs: project_kernel(radius, *refs),
        "project",
        shapes((owned, 2, wide, DEGREES // 2), F32),
        [
            pltpu.VMEM(((places + 2 * radius) * owned, lanes), F32),
            pltpu.VMEM((places * owned, lanes), F32),
            pltpu.VMEM((slots, 2, wide, DEGREES // 2), F32),
            pltpu.SemaphoreType.DMA((slots,)),
        ],
        6,
        2 * owned * wide * places * ((taps + 1) * wide + DEGREES),
        (got, table),
        out_specs=HBM,
    )
    return spectrum.reshape(owned, 2, channels, 2, DEGREES // 2)


def solution(mesh):
    placed = (
        P("chan", "lat", None),
        P("chan", None, None, None),
        P("chan"),
        P("chan", None, None, None),
    )
    return jax.shard_map(
        per_device,
        mesh=mesh,
        in_specs=placed,
        out_specs=P("lat", None, "chan", None, None),
        check_vma=False,
    )
```

time: 62.6 us -> 39 us (0.62)
  blocking collectives: 12.3 us -> 0 us
  local copies, waits for them, and re-layouts: 11.5 us -> 4.45 us
  Pallas kernels: 24.8 us -> 19.7 us
  waiting for transfers between devices: 2.14 us -> 6.11 us
  starting transfers between devices: 11.1 us -> 8.26 us
    all_to_all x1 -> x0, blocking collectives: 12.3 us -> none  [per_device(): got_inner = lax.all_to_all(send_inner, 'lat', 0, 0, tiled=True)]
    pallas_call x4 -> x5, Pallas kernels: 24.8 us -> 19.7 us  [call(): pl.pallas_call(kernel, out_shape=out_shape, in_specs=in_specs or [VMEM] *...]
    all_to_all x2 -> x1, waiting for transfers between devices: 2.14 us -> 6.11 us  [per_device(): got = lax.all_to_all(send, 'lat', 0, 0, tiled=True)]
    unnamed x20 -> x10, local copies, waits for them, and re-layouts: 7.08 us -> 3.73 us
    all_to_all x2 -> x1, starting transfers between devices: 7.41 us -> 4.16 us  [per_device(): got = lax.all_to_all(send, 'lat', 0, 0, tiled=True)]
    slice x1 -> x0, local copies, waits for them, and re-layouts: 2.51 us -> none  [per_device(): first = atmosphere[:, :radius].reshape(channels * radius, length)]
    reshape x2 -> x0, local copies, waits for them, and re-layouts: 1.79 us -> none  [the longest x1 0.9 us: per_device(): first = atmosphere[:, :radius].reshape(channels * radius, length)]
    broadcast_in_dim x1, local copies, waits for them, and re-layouts: 0.07 us -> 0.72 us  [per_device(): bias = jnp.broadcast_to(first_bias[:, None], (channels, LANES))]
  transfers between devices with their start and end apart: 4 -> 3, of which waited for: 1 -> 1; matrix products, arithmetic and copies ran while one was open for 2% -> 2% of each run, Pallas kernels for 30% -> 25%
where the time goes in v2:
time: 39 us; the launch traced here: 38.7 us
  Pallas kernels  19.7 us (51%)
  starting transfers between devices  8.26 us (21%)
  waiting for transfers between devices  6.11 us (16%)
  local copies, waits for them, and re-layouts  4.45 us (11%)
    pallas_call x5, Pallas kernels, call(): pl.pallas_call(kernel, out_shape=out_shape, in_specs=in_specs or [VMEM] *...  19.7 us
    all_to_all x1, waiting for transfers between devices, per_device(): got = lax.all_to_all(send, 'lat', 0, 0, tiled=True)  6.11 us
    all_to_all x1, starting transfers between devices, per_device(): got = lax.all_to_all(send, 'lat', 0, 0, tiled=True)  4.16 us
    unnamed x10, local copies, waits for them, and re-layouts  3.73 us
    ppermute x1, starting transfers between devices, per_device(): cross = lax.ppermute(cross, 'lat', crosses)  3.55 us
  transfers between devices with their start and end apart: 3, of which 1 were waited for; matrix products, arithmetic and copies ran while one was open for 2% of the time, Pallas kernels for 25%

profile of v2, /device:TPU:0, one launch (start us, length us, event | category | flops | bytes accessed | tf_op | source)
XLA Modules:
  0.0 38.7 jit_solution(7241532141790563459)
XLA Ops:
  0.0 0.0 copy-start
  0.0 1.4 %copy-done = bf16[64,8,1536]{2,1,0:T(8,128)(2,1)S(1)} copy-done((bf16[64,8,1536]{2,1,0:T(8,128)(2,1)S(1)}, bf16[64,8,1536]{2,1,0:T(8,128)(2,1)}, u32[]{:S(2)}) %copy-start) | copy-done | bytes 1572888
  1.4 0.4 edges.1
  1.8 0.6 %collective-permute-start = (bf16[128,1536]{1,0:T(8,128)(2,1)S(1)}, bf16[128,1536]{1,0:T(8,128)(2,1)S(1)}, u32[]{:S(2)}, u32[]{:S(2)}) collective-permute-start(bf16[128,1536]{1,0:T(8,128)(2,1)S(1)} %get-tuple-element.13), channel_id=1, source_target_pairs={{0,4},{4,0},{8,12},{12,8},{16,20},{20,16},{24,28},{28,24},{1,5},{5... | collective-permute-start | bytes 1179656 | tf_op jit(solution)/shard_map/ppermute | solution.py:418
  2.3 3.5 %collective-permute-start.1 = (bf16[128,1536]{1,0:T(8,128)(2,1)S(1)}, bf16[128,1536]{1,0:T(8,128)(2,1)S(1)}, u32[]{:S(2)}, u32[]{:S(2)}) collective-permute-start(bf16[128,1536]{1,0:T(8,128)(2,1)S(1)} %get-tuple-element.14), channel_id=1, source_target_pairs={{0,28},{4,8},{8,4},{12,16},{16,12},{20,24},{24,20},{28,0},{1,29},{... | collective-permute-start | bytes 1179656 | tf_op jit(solution)/shard_map/ppermute | solution.py:417
  5.9 0.7 %broadcast_in_dim.2.refs_1_ = f32[64,128]{1,0:T(8,128)S(1)} broadcast(f32[64]{0:T(128)} %param.7), dimensions={0} | broadcast | bytes 33024 | tf_op jit(solution)/shard_map/broadcast_in_dim | solution.py:420
  6.6 0.0 copy-start.1
  6.6 1.4 %copy-done.1 = bf16[64,8,1536]{2,1,0:T(8,128)(2,1)S(1)} copy-done((bf16[64,8,1536]{2,1,0:T(8,128)(2,1)S(1)}, bf16[64,8,1536]{2,1,0:T(8,128)(2,1)}, u32[]{:S(2)}) %copy-start.1) | copy-done | bytes 1572888
  8.0 0.0 copy-start.4
  8.0 0.9 %copy-done.4 = bf16[64,16,5,5]{0,1,3,2:T(8,128)(2,1)S(1)} copy-done((bf16[64,16,5,5]{0,1,3,2:T(8,128)(2,1)S(1)}, bf16[64,16,5,5]{0,1,3,2:T(8,128)(2,1)}, u32[]{:S(2)}) %copy-start.4) | copy-done | bytes 51224
  8.9 6.2 %interior.1 = (f32[4,64,1536]{2,1,0:T(8,128)S(1)}, bf16[1280,32]{1,0:T(8,128)(2,1)S(1)}, bf16[1536,256]{1,0:T(8,128)(2,1)S(1)}, bf16[8,12,16,128]{3,2,1,0:T(8,128)(2,1)S(1)}) custom-call(bf16[5,5,16,64]{3,2,1,0:T(8,128)(2,1)S(1)} %bitcast.7, f32[64,128]{1,0:T(8,128)S(1)} %broadcast_in_dim.2.refs_1_, bf16[512,1536]{1,0:T(8,128)(2,1)S(1)} %bitcast.5), custom_call_target="tpu_custom_call" | custom-call | flops 1006632960 | bytes 4491264 | tf_op jit(solution)/shard_map/interior/pallas_call | solution.py:49
  15.2 0.0 collective-permute-done.refs_2_
  15.2 0.0 collective-permute-done.1.refs_3_
  15.2 0.0 copy-start.2
  15.2 0.0 copy-start.3
  15.2 3.9 %rim.1 = bf16[8,16,16,128]{3,2,1,0:T(8,128)(2,1)} custom-call(bf16[1280,32]{1,0:T(8,128)(2,1)S(1)} %get-tuple-element.11.refs_0_, f32[4,64,1536]{2,1,0:T(8,128)S(1)} %get-tuple-element.12.refs_1_, bf16[128,1536]{1,0:T(8,128)(2,1)S(1)} %collective-permute-done.refs_2_, bf16[128,1536]{1,0:T(8,128)(2,1)S(1)} %collective-permute-done.1.refs_3_, ...), custom_call_target="tpu_custom_call" | custom-call | flops 125829120 | bytes 4145152 | tf_op jit(solution)/shard_map/rim/pallas_call | solution.py:49
  19.1 4.2 %all-to-all-start = ((bf16[8,16,16,128]{3,2,1,0:T(8,128)(2,1)}), bf16[8,16,16,128]{3,2,1,0:T(8,128)(2,1)}, u32[]{:S(2)}, u32[]{:S(2)}) async-start(bf16[8,16,16,128]{3,2,1,0:T(8,128)(2,1)} %rim.1), calls=%async_computation | async-start | bytes 1048576 | tf_op jit(solution)/shard_map/all_to_all | solution.py:452
  23.4 0.0 copy-done.2
  23.4 0.0 copy-done.3
  23.4 3.5 %tables.1.refs_1_ = bf16[16,128,768]{2,1,0:T(8,128)(2,1)S(1)} custom-call(f32[4,16]{1,0:T(4,128)S(1)} %pad_maximum_fusion.refs_0_, f32[3,8,128]{2,1,0:T(8,128)S(1)} %copy-done.3, bf16[5,5,16,64]{3,2,1,0:T(8,128)(2,1)S(1)} %bitcast.6), custom_call_target="tpu_custom_call" | custom-call | flops 20971520 | bytes 3209472 | tf_op jit(solution)/shard_map/tables/pallas_call | solution.py:49
  26.9 6.1 %all-to-all-done.refs_0_ = bf16[8,16,16,128]{3,2,1,0:T(8,128)(2,1)} async-done(((bf16[8,16,16,128]{3,2,1,0:T(8,128)(2,1)}), bf16[8,16,16,128]{3,2,1,0:T(8,128)(2,1)}, u32[]{:S(2)}, u32[]{:S(2)}) %all-to-all-start) | async-done | bytes 524320 | tf_op jit(solution)/shard_map/all_to_all | solution.py:452
  33.0 5.7 %project.1 = f32[16,2,128,128]{3,2,1,0:T(8,128)} custom-call(bf16[8,16,16,128]{3,2,1,0:T(8,128)(2,1)} %all-to-all-done.refs_0_, bf16[16,128,768]{2,1,0:T(8,128)(2,1)S(1)} %tables.1.refs_1_), custom_call_target="tpu_custom_call" | custom-call | flops 268435456 | bytes 5767168 | tf_op jit(solution)/shard_map/project/pallas_call | solution.py:49
  (3 shorter events, 0.1 us)
Async XLA Ops:
  0.0 1.4 %copy-start = (bf16[64,8,1536]{2,1,0:T(8,128)(2,1)S(1)}, bf16[64,8,1536]{2,1,0:T(8,128)(2,1)}, u32[]{:S(2)}) copy-start(bf16[64,8,1536]{2,1,0:T(8,128)(2,1)} %param.5) | copy-start | bytes 4718596
  1.8 13.4 %collective-permute-start = (bf16[128,1536]{1,0:T(8,128)(2,1)S(1)}, bf16[128,1536]{1,0:T(8,128)(2,1)S(1)}, u32[]{:S(2)}, u32[]{:S(2)}) collective-permute-start(bf16[128,1536]{1,0:T(8,128)(2,1)S(1)} %get-tuple-element.13), channel_id=1, source_target_pairs={{0,4},{4,0},{8,12},{12,8},{16,20},{20,16},{24,28},{28,24},{1,5},{5... | collective-permute-start | bytes 1179656 | tf_op jit(solution)/shard_map/ppermute | solution.py:418
  2.3 12.8 %collective-permute-start.1 = (bf16[128,1536]{1,0:T(8,128)(2,1)S(1)}, bf16[128,1536]{1,0:T(8,128)(2,1)S(1)}, u32[]{:S(2)}, u32[]{:S(2)}) collective-permute-start(bf16[128,1536]{1,0:T(8,128)(2,1)S(1)} %get-tuple-element.14), channel_id=1, source_target_pairs={{0,28},{4,8},{8,4},{12,16},{16,12},{20,24},{24,20},{28,0},{1,29},{... | collective-permute-start | bytes 1179656 | tf_op jit(solution)/shard_map/ppermute | solution.py:417
  6.6 1.4 %copy-start.1 = (bf16[64,8,1536]{2,1,0:T(8,128)(2,1)S(1)}, bf16[64,8,1536]{2,1,0:T(8,128)(2,1)}, u32[]{:S(2)}) copy-start(bf16[64,8,1536]{2,1,0:T(8,128)(2,1)} %param.5) | copy-start | bytes 4718596
  8.0 0.9 %copy-start.4 = (bf16[64,16,5,5]{0,1,3,2:T(8,128)(2,1)S(1)}, bf16[64,16,5,5]{0,1,3,2:T(8,128)(2,1)}, u32[]{:S(2)}) copy-start(bf16[64,16,5,5]{0,1,3,2:T(8,128)(2,1)} %param.6) | copy-start | bytes 153604
  15.2 8.2 %copy-start.2 = (bf16[64,16,5,5]{0,1,3,2:T(8,128)(2,1)S(1)}, bf16[64,16,5,5]{0,1,3,2:T(8,128)(2,1)}, u32[]{:S(2)}) copy-start(bf16[64,16,5,5]{0,1,3,2:T(8,128)(2,1)} %param.8) | copy-start | bytes 153604
  15.2 8.2 %copy-start.3 = (f32[3,8,128]{2,1,0:T(8,128)S(1)}, f32[3,8,128]{2,1,0:T(8,128)}, u32[]{:S(2)}) copy-start(f32[3,8,128]{2,1,0:T(8,128)} %constant.17.clone.refs_1_) | copy-start | bytes 36868
  19.1 13.9 %all-to-all-start = ((bf16[8,16,16,128]{3,2,1,0:T(8,128)(2,1)}), bf16[8,16,16,128]{3,2,1,0:T(8,128)(2,1)}, u32[]{:S(2)}, u32[]{:S(2)}) async-start(bf16[8,16,16,128]{3,2,1,0:T(8,128)(2,1)} %rim.1), calls=%async_computation | async-start | bytes 1048576 | tf_op jit(solution)/shard_map/all_to_all | solution.py:452

commit v3 on v2

--- a/solution.py
+++ b/solution.py
@@ -107,27 +107,39 @@
     return total
 
 
-def edges_kernel(group, radius, groups, field_ref, pair_ref, cross_ref):
+def picked(group, radius, groups, field_ref, crossing):
     block = field_ref.shape[0] // groups
     height = block // group
     depth = radius * group
-    parity = lax.axis_index("lat") % 2
-    shape = (2 * depth, block)
+    shape = (depth, block)
     place, column = iota(shape, 0), iota(shape, 1)
-    far = (place // depth + parity) % 2 == 0
+    far = (lax.axis_index("lat") + crossing) % 2 == 0
     row = place % radius + jnp.where(far, height - radius, 0)
-    chosen = column == place % depth // radius * height + row
+    chosen = column == place // radius * height + row
     selector = chosen.astype(F32).astype(BF16)
     for g in range(groups):
-        found = dot_nn(selector, field_ref[g * block : (g + 1) * block, :]).astype(BF16)
-        pair_ref[g * depth : (g + 1) * depth, :] = found[:depth, :]
-        cross_ref[g * depth : (g + 1) * depth, :] = found[depth:, :]
+        yield dot_nn(selector, field_ref[g * block : (g + 1) * block, :]).astype(BF16)
+
+
+def cross_kernel(group, radius, groups, field_ref, kept_ref, *cross_refs):
+    share = groups // len(cross_refs)
+    depth = radius * group
+    for g, rows in enumerate(picked(group, radius, groups, field_ref, 1)):
+        start = g % share * depth
+        cross_refs[g // share][start : start + depth, :] = rows
+    kept_ref[...] = field_ref[...]
+
+
+def pair_kernel(group, radius, groups, field_ref, pair_ref):
+    depth = radius * group
+    for g, rows in enumerate(picked(group, radius, groups, field_ref, 0)):
+        pair_ref[g * depth : (g + 1) * depth, :] = rows
 
 
 def interior_kernel(
     group, weight_ref, bias_ref, field_ref,
     edge_ref, rim_ref, fourier_ref, send_ref,
-    band_ref, partial_ref, hidden_ref, spectra_ref,
+    band_ref, partial_ref, hidden_ref, spectra_ref, column_ref,
 ):
     taps = weight_ref.shape[0]
     radius = taps // 2
@@ -140,16 +152,24 @@
     rows = taps * block
 
     write_fourier(fourier_ref, field_ref.shape[1], orders)
+    shape = (channels, channels)
+    bias = jnp.where(iota(shape, 0) == iota(shape, 1), bias_ref[...], 0.0)
+    column_ref[...] = jnp.broadcast_to(jnp.sum(bias, axis=1, keepdims=True), column_ref.shape)
     shape = (taps * group, height * block)
     place = iota(shape, 0)
     column = iota(shape, 1)
     out_row, column = column // block, column % block
     chosen = (place % group == column // height) & (place // group == column % height - out_row + radius)
     selector = chosen.astype(F32).astype(BF16)
-    rim_shape = (taps * group, radius * group)
+    position = lax.axis_index("lat")
+    parity = position % 2
+    polar = (position == 0) | (position == lax.axis_size("lat") - 1)
+    open_side = jnp.where(polar, 0.0, 1.0)
+    depth = radius * group
+    rim_shape = (taps * group, 2 * depth)
     rim_place = iota(rim_shape, 0)
     rim_column = iota(rim_shape, 1)
-    same = rim_place % group == rim_column // radius
+    same = rim_place % group == rim_column % depth // radius
     rim_row = rim_column % radius
     rim_rows = taps * radius * group
     for dx in range(taps):
@@ -161,13 +181,15 @@
                 band_ref[start : start + group, :] = spread[
                     g * group : (g + 1) * group, row * block : (row + 1) * block
                 ]
-        for side in range(2):
+        for which in range(2):
+            side = 1 - parity if which == 0 else parity
             for row in range(radius):
-                tap = rim_row - row + (0 if side == 0 else taps - 1)
-                pick = (same & (rim_place // group == tap)).astype(F32).astype(BF16)
-                spread = dot_tn(mine, pick).astype(BF16)
+                tap = rim_row - row + side * (taps - 1)
+                own = same & (rim_column // depth == which) & (rim_place // group == tap)
+                pick = jnp.where(own, 1.0 if which == 0 else open_side, 0.0)
+                spread = dot_tn(mine, pick.astype(BF16)).astype(BF16)
                 for g in range(groups):
-                    start = (g * 2 + side) * rim_rows + (dx * radius + row) * group
+                    start = (g * 2 + which) * rim_rows + (dx * radius + row) * group
                     rim_ref[start : start + group, :] = spread[g * group : (g + 1) * group, :]
 
     def per_group(g, carry):
@@ -175,7 +197,7 @@
         field = field_ref[pl.ds(pl.multiple_of(g * block, 16), block), :]
         partial_ref[...] = dot_nn(band, field)
         mine = pl.ds(pl.multiple_of(g * group, 16), group)
-        bias = bias_ref[mine, :][:, :1]
+        bias = column_ref[mine, :][:, :1]
         for row in range(height):
             total = shifted_sum(partial_ref, rows, block, row * group, group) + bias
             if radius <= row < height - radius:
@@ -188,12 +210,17 @@
     lax.fori_loop(0, groups, per_group, 0)
 
     found = dot_nn(field_ref[...], fourier_ref[...])
-    total = height * channels
+    pitch = height + 1
+    total = pitch * channels
     for part in range(2):
-        spectra_ref[part * total : (part + 1) * total, :] = found[:, part * orders : (part + 1) * orders]
+        for channel in range(channels):
+            start = part * total + channel * pitch
+            spectra_ref[start : start + height, :] = found[
+                channel * height : (channel + 1) * height, part * orders : (part + 1) * orders
+            ]
     for row in range(height):
         real, imaginary = (
-            spectra_ref[pl.ds(part * total + row, channels, stride=height), :] for part in range(2)
+            spectra_ref[pl.ds(part * total + row, channels, stride=pitch), :] for part in range(2)
         )
         write_spectra(send_ref, row, real, imaginary)
     found = dot_nn(hidden_ref[...], fourier_ref[...])
@@ -202,41 +229,63 @@
         write_spectra(send_ref, height + row, mine[:, :orders], mine[:, orders:])
 
 
-def rim_kernel(
-    group, radius, rim_ref, edge_ref, pair_ref, cross_ref, fourier_ref, early_ref,
-    send_ref, partial_ref, hidden_ref,
-):
-    channels = edge_ref.shape[1]
-    groups = channels // group
-    orders = fourier_ref.shape[1] // 2
+def write_rim(group, radius, groups, rim_ref, edge_ref, pair_ref, cross_ref, partial_ref, store):
     rows = partial_ref.shape[0]
     depth = radius * group
-    early = early_ref.shape[1]
-    position = lax.axis_index("lat")
-    parity = position % 2
-    polar = (position == 0) | (position == lax.axis_size("lat") - 1)
-
-    def per_group(g, carry):
-        for halo_ref, side in ((pair_ref, 1 - parity), (cross_ref, parity)):
-            rim = rim_ref[pl.ds(pl.multiple_of((g * 2 + side) * rows, 16), rows), :]
-            if halo_ref is cross_ref:
-                rim = jnp.where(polar, jnp.zeros_like(rim), rim)
-            halo = halo_ref[pl.ds(pl.multiple_of(g * depth, 16), depth), :]
-            partial_ref[...] = dot_nn(rim, halo)
+    parity = lax.axis_index("lat") % 2
+
+    def per_group(at, carry):
+        g = groups[0] + at
+        rim = rim_ref[pl.ds(pl.multiple_of(g * rows, 16), rows), :]
+        pair = pair_ref[pl.ds(pl.multiple_of(g * depth, 16), depth), :]
+        cross = cross_ref[pl.ds(pl.multiple_of(at * depth, 16), depth), :]
+        partial_ref[...] = dot_nn(rim, jnp.concatenate([pair, cross], axis=0))
+        for which, side in ((0, 1 - parity), (1, parity)):
+            mine_ref = partial_ref.at[which * rows // 2 : (which + 1) * rows // 2]
             for row in range(radius):
-                total = shifted_sum(partial_ref, rows, depth, row * group, group)
+                total = shifted_sum(mine_ref, rows // 2, depth, row * group, group)
                 place = side * radius + row
                 total = total + edge_ref[place, pl.ds(pl.multiple_of(g * group, 16), group), :]
-                start = pl.multiple_of(place * channels + g * group, 16)
-                hidden_ref[pl.ds(start, group), :] = gelu(total).astype(BF16)
+                store(place, g, at, gelu(total).astype(BF16))
         return carry
 
-    lax.fori_loop(0, groups, per_group, 0)
-    send_ref[:, :early] = early_ref[...]
+    lax.fori_loop(0, groups[1] - groups[0], per_group, 0)
+
+
+def first_rim_kernel(group, radius, groups, rim_ref, edge_ref, pair_ref, cross_ref, hidden_ref, partial_ref):
+    def store(place, g, at, value):
+        hidden_ref[place, pl.ds(pl.multiple_of(at * group, 16), group), :] = value
+
+    write_rim(group, radius, groups, rim_ref, edge_ref, pair_ref, cross_ref, partial_ref, store)
+
+
+def last_rim_kernel(
+    group, radius, groups, rim_ref, edge_ref, pair_ref, cross_ref, fourier_ref, early_ref, *refs
+):
+    before_refs, (send_hbm, partial_ref, hidden_ref, late_ref, semaphores) = refs[:-5], refs[-5:]
+    channels = edge_ref.shape[1]
+    orders = fourier_ref.shape[1] // 2
+    early = early_ref.shape[1]
+    first = pltpu.make_async_copy(early_ref, send_hbm.at[:, pl.ds(0, early)], semaphores.at[0])
+    first.start()
+    for place in range(2 * radius):
+        for before_ref in before_refs:
+            size = before_ref.shape[1]
+            hidden_ref[place * channels : place * channels + size, :] = before_ref[place]
+
+    def store(place, g, at, value):
+        start = pl.multiple_of(place * channels + g * group, 16)
+        hidden_ref[pl.ds(start, group), :] = value
+
+    write_rim(group, radius, groups, rim_ref, edge_ref, pair_ref, cross_ref, partial_ref, store)
     found = dot_nn(hidden_ref[...], fourier_ref[...])
     for row in range(2 * radius):
         mine = found[row * channels : (row + 1) * channels, :]
-        write_spectra(send_ref, early + row, mine[:, :orders], mine[:, orders:])
+        write_spectra(late_ref, row, mine[:, :orders], mine[:, orders:])
+    last = pltpu.make_async_copy(late_ref, send_hbm.at[:, pl.ds(early, 2 * radius)], semaphores.at[1])
+    last.start()
+    first.wait()
+    last.wait()
 
 
 def tables_kernel(
@@ -284,16 +333,16 @@
     across = (iota((group, wide), 1) % group == iota((group, wide), 0)).astype(F32).astype(BF16)
     shape = (wide, wide)
     row, column = iota(shape, 0), iota(shape, 1)
-    row_part, column_part = row % 2, column // channels
-    same_group = row // 2 // group == column % channels // group
+    row_part, column_part = row // channels, column % 2
+    same_group = row % channels // group == column // 2 // group
     straight = row_part == column_part
-    sign = jnp.where(row_part > column_part, 1.0, -1.0)
+    sign = jnp.where(column_part > row_part, 1.0, -1.0)
     flat = jnp.concatenate([weight_ref[dy, dx] for dy in range(taps) for dx in range(taps)], axis=0)
     doubled = dot_nn(flat, twice).astype(BF16)
 
     def expanded(dy, dx):
         start = (dy * taps + dx) * group
-        return dot_tn(doubled[start : start + group, :], across)
+        return dot_tn(across, doubled[start : start + group, :])
 
     for dy in range(taps):
         tap = [expanded(dy, dx) for dx in range(taps)]
@@ -320,7 +369,7 @@
             total = base_ref[dy, 0]
             for far in range(radius):
                 total = total + base_ref[dy, far + 1] * factors[far]
-            table_ref[k, :wide, dy * wide : (dy + 1) * wide] = total.astype(BF16)
+            table_ref[k, dy * wide : (dy + 1) * wide, :wide] = total.astype(BF16)
         return latest, before
 
     nothing = order * cosine * 0.0
@@ -334,8 +383,8 @@
     for parity in range(2):
         for k in range(owned):
             mine = turned_ref[pl.ds(parity * total + k, places, stride=owned), :]
-            rows = slice(parity * places, (parity + 1) * places)
-            table_ref[k, rows, taps * wide :] = mine.astype(BF16)
+            start = taps * wide + parity * places
+            table_ref[k, start : start + places, :half] = mine.astype(BF16)
 
 
 def project_kernel(
@@ -344,15 +393,15 @@
     members, height, owned, wide = got_ref.shape
     height = height // 2
     places = members * height
-    pad = radius * owned
+    pitch = owned + 1
+    pad = radius * pitch
     taps = 2 * radius + 1
-    slots = out_ref.shape[0]
 
     rows_ref[:pad, :] = jnp.zeros((pad, rows_ref.shape[1]), F32)
-    rows_ref[pad + places * owned :, :] = jnp.zeros((pad, rows_ref.shape[1]), F32)
+    rows_ref[pad + places * pitch :, :] = jnp.zeros((pad, rows_ref.shape[1]), F32)
     for source in range(members):
         for row in range(height):
-            start = (source * height + row) * owned
+            start = (source * height + row) * pitch
             plain_ref[start : start + owned, :wide] = got_ref[source, row].astype(F32)
             if radius <= row < height - radius:
                 place = height + row - radius
@@ -363,26 +412,37 @@
             rows_ref[pad + start : pad + start + owned, :wide] = got_ref[source, place].astype(F32)
 
     row, column = iota((wide, wide), 0), iota((wide, wide), 1)
-    identity = (column == row % 2 * (wide // 2) + row // 2).astype(F32).astype(BF16)
-
-    def sent(k, slot):
-        return pltpu.make_async_copy(out_ref.at[slot], out_hbm.at[k], semaphores.at[slot])
-
+    identity = (row == column % 2 * (wide // 2) + column // 2).astype(F32).astype(BF16)
+    identity = jnp.concatenate([identity] * (2 if owned % 2 == 0 else 1), axis=1)
+    mix = taps * wide
+    half = out_ref.shape[3]
+
+    def sent(k):
+        return pltpu.make_async_copy(out_ref.at[k], out_hbm.at[k], semaphores.at[k])
+
+    def gathered(k):
+        pieces = [rows_ref[pl.ds(dy * pitch + k, places, stride=pitch), :] for dy in range(taps)]
+        pieces.append(plain_ref[pl.ds(k, places, stride=pitch), :])
+        return jnp.concatenate([piece[:, :wide].astype(BF16) for piece in pieces], axis=1)
+
+    together = 2 if owned % 2 == 0 else 1
+    for first in range(0, owned, together):
+        orders = range(first, first + together)
+        stacked = jnp.concatenate([gathered(k) for k in orders], axis=0)
+        mixing = jnp.concatenate([table_ref[k, :mix, :wide] for k in orders], axis=1)
+        mixing = jnp.concatenate([mixing, identity], axis=0)
+        both = dot_nn(stacked, mixing)
+        for at, k in enumerate(orders):
+            mixed = both[at * places : (at + 1) * places, at * wide : (at + 1) * wide].T.astype(BF16)
+            legendre = jnp.concatenate(
+                [table_ref[k, mix + q * places : mix + (q + 1) * places, :half] for q in range(2)], axis=1
+            )
+            found = dot_nn(mixed, legendre)
+            out_ref[k, 0] = found[:, :half]
+            out_ref[k, 1] = found[:, half:]
+            sent(k).start()
     for k in range(owned):
-        slot = k % slots
-        pieces = [rows_ref[pl.ds(dy * owned + k, places, stride=owned), :] for dy in range(taps)]
-        pieces.append(plain_ref[pl.ds(k, places, stride=owned), :])
-        stacked = jnp.concatenate([piece[:, :wide].astype(BF16) for piece in pieces], axis=1)
-        mixing = jnp.concatenate([table_ref[k, :wide, : taps * wide], identity], axis=1)
-        mixed = dot_nt(mixing, stacked).astype(BF16)
-        if k >= slots:
-            sent(k - slots, slot).wait()
-        for parity in range(2):
-            rows = slice(parity * places, (parity + 1) * places)
-            out_ref[slot, parity] = dot_nn(mixed, table_ref[k, rows, taps * wide :])
-        sent(k, slot).start()
-    for k in range(max(0, owned - slots), owned):
-        sent(k, k % slots).wait()
+        sent(k).wait()
 
 
 def per_device(atmosphere, first_weight, first_bias, second_weight):
@@ -403,27 +463,38 @@
     first_taps = first_weight.transpose(2, 3, 1, 0)
     second_taps = second_weight.transpose(2, 3, 1, 0)
     flat = atmosphere.reshape(channels * height, length)
-    pair, cross = call(
-        lambda *refs: edges_kernel(group, radius, groups, *refs),
-        "edges",
-        (shapes((channels * radius, length), BF16), shapes((channels * radius, length), BF16)),
+    shares = 2 if groups % 2 == 0 else 1
+    share = groups // shares
+    part = shapes((share * group * radius, length), BF16)
+    flat, *crossed = call(
+        lambda *refs: cross_kernel(group, radius, groups, *refs),
+        "cross_rows",
+        (shapes(flat.shape, BF16),) + (part,) * shares,
         [],
-        8,
-        4 * radius * channels * block * length,
+        6,
+        2 * radius * channels * block * length,
         (flat,),
     )
+    crosses = [(i, (i + 1 if i % 2 else i - 1) % members) for i in range(members)]
+    crossed = [lax.ppermute(cross, "lat", crosses) for cross in crossed]
+    pair = call(
+        lambda *refs: pair_kernel(group, radius, groups, *refs),
+        "pair_rows",
+        shapes((channels * radius, length), BF16),
+        [],
+        6,
+        2 * radius * channels * block * length,
+        (flat,),
+    )
     pairs = [(i, i ^ 1) for i in range(members) if i ^ 1 < members]
-    crosses = [(i, (i + 1 if i % 2 else i - 1) % members) for i in range(members)]
-    cross = lax.ppermute(cross, "lat", crosses)
     pair = lax.ppermute(pair, "lat", pairs)
 
-    bias = jnp.broadcast_to(first_bias[:, None], (channels, LANES))
     edge, rim, fourier, early = call(
         lambda *refs: interior_kernel(group, *refs),
         "interior",
         (
             shapes((2 * radius, channels, length), F32),
-            shapes((groups * 2 * rim_rows, radius * group), BF16),
+            shapes((groups * 2 * rim_rows, 2 * radius * group), BF16),
             shapes((length, 2 * ORDERS), BF16),
             shapes((members, height + inner, owned, wide), BF16),
         ),
@@ -431,23 +502,41 @@
             pltpu.VMEM((groups * taps * block, block), BF16),
             pltpu.VMEM((taps * block, length), F32),
             pltpu.VMEM((inner * channels, length), BF16),
-            pltpu.VMEM((2 * height * channels, ORDERS), F32),
+            pltpu.VMEM((2 * (height + 1) * channels, ORDERS), F32),
+            pltpu.VMEM((channels, LANES), F32),
         ],
         10,
         2 * taps * block * block * length * groups,
-        (first_taps, bias, flat),
-    )
+        (first_taps, first_bias[None, :], flat),
+    )
+    partial = pltpu.VMEM((2 * rim_rows, length), F32)
+    flops = 8 * rim_rows * radius * group * length * share
+    before = [
+        call(
+            lambda *refs: first_rim_kernel(group, radius, (0, share), *refs),
+            "rim_first",
+            shapes((2 * radius, share * group, length), BF16),
+            [partial],
+            6,
+            flops,
+            (rim, edge, pair, cross),
+        )
+        for cross in crossed[:-1]
+    ]
     send = call(
-        lambda *refs: rim_kernel(group, radius, *refs),
-        "rim",
+        lambda *refs: last_rim_kernel(group, radius, (groups - share, groups), *refs),
+        "rim_last",
         shapes((members, 2 * height, owned, wide), BF16),
         [
-            pltpu.VMEM((rim_rows, length), F32),
+            partial,
             pltpu.VMEM((2 * radius * channels, length), BF16),
+            pltpu.VMEM((members, 2 * radius, owned, wide), BF16),
+            pltpu.SemaphoreType.DMA((2,)),
         ],
-        6,
-        2 * groups * 2 * rim_rows * radius * group * length,
-        (rim, edge, pair, cross, fourier, early),
+        8,
+        flops,
+        (rim, edge, pair, crossed[-1], fourier, early, *before),
+        out_specs=HBM,
     )
     got = lax.all_to_all(send, "lat", 0, 0, tiled=True)
 
@@ -463,7 +552,7 @@
     table = call(
         lambda *refs: tables_kernel(group, *refs),
         "tables",
-        shapes((owned, max(wide, 2 * places), taps * wide + DEGREES // 2), BF16),
+        shapes((owned, taps * wide + 2 * places, max(wide, DEGREES // 2)), BF16),
         [
             pltpu.VMEM((DEGREES * head, LANES), F32),
             pltpu.VMEM((2 * DEGREES, LANES), F32),
@@ -477,16 +566,15 @@
     )
 
     lanes = max(wide, LANES)
-    slots = owned
     spectrum = call(
         lambda *refs: project_kernel(radius, *refs),
         "project",
         shapes((owned, 2, wide, DEGREES // 2), F32),
         [
-            pltpu.VMEM(((places + 2 * radius) * owned, lanes), F32),
-            pltpu.VMEM((places * owned, lanes), F32),
-            pltpu.VMEM((slots, 2, wide, DEGREES // 2), F32),
-            pltpu.SemaphoreType.DMA((slots,)),
+            pltpu.VMEM(((places + 2 * radius) * (owned + 1), lanes), F32),
+            pltpu.VMEM((places * (owned + 1), lanes), F32),
+            pltpu.VMEM((owned, 2, wide, DEGREES // 2), F32),
+            pltpu.SemaphoreType.DMA((owned,)),
         ],
         6,
         2 * owned * wide * places * ((taps + 1) * wide + DEGREES),

time: 39 us -> 36 us (0.923)
  local copies, waits for them, and re-layouts: 4.45 us -> 1.42 us
  waiting for transfers between devices: 6.11 us -> 7.67 us
  Pallas kernels: 19.7 us -> 18.2 us
    unnamed x10, local copies, waits for them, and re-layouts: 3.73 us -> 1.42 us
    pallas_call x5 -> x7, Pallas kernels: 19.7 us -> 18.2 us  [call(): pl.pallas_call(kernel, out_shape=out_shape, in_specs=in_specs or [VMEM] *...]
    ppermute x1 -> x2, waiting for transfers between devices: 0.01 us -> 1.27 us  [per_device(): crossed = [lax.ppermute(cross, 'lat', crosses) for cross in crossed]]
    broadcast_in_dim x1 -> x0, local copies, waits for them, and re-layouts: 0.72 us -> none  [per_device(): bias = jnp.broadcast_to(first_bias[:, None], (channels, LANES))]
    ppermute x1 -> x2, starting transfers between devices: 3.55 us -> 3.58 us  [per_device(): crossed = [lax.ppermute(cross, 'lat', crosses) for cross in crossed]]
  transfers between devices with their start and end apart: 3 -> 4, of which waited for: 1 -> 2; matrix products, arithmetic and copies ran while one was open for 2% -> 0% of each run, Pallas kernels for 25% -> 30%
where the time goes in v3:
time: 36 us; the launch traced here: 35.8 us
  Pallas kernels  18.2 us (51%)
  starting transfers between devices  8.3 us (23%)
  waiting for transfers between devices  7.67 us (21%)
  local copies, waits for them, and re-layouts  1.42 us (4%)
    pallas_call x7, Pallas kernels, call(): pl.pallas_call(kernel, out_shape=out_shape, in_specs=in_specs or [VMEM] *...  18.2 us
    all_to_all x1, waiting for transfers between devices, per_device(): got = lax.all_to_all(send, 'lat', 0, 0, tiled=True)  6.4 us
    all_to_all x1, starting transfers between devices, per_device(): got = lax.all_to_all(send, 'lat', 0, 0, tiled=True)  4.16 us
    ppermute x2, starting transfers between devices, per_device(): crossed = [lax.ppermute(cross, 'lat', crosses) for cross in crossed]  3.58 us
    unnamed x10, local copies, waits for them, and re-layouts  1.42 us
    ppermute x2, waiting for transfers between devices, per_device(): crossed = [lax.ppermute(cross, 'lat', crosses) for cross in crossed]  1.27 us
  transfers between devices with their start and end apart: 4, of which 2 were waited for; matrix products, arithmetic and copies ran while one was open for 0% of the time, Pallas kernels for 30%

profile of v3, /device:TPU:0, one launch (start us, length us, event | category | flops | bytes accessed | tf_op | source)
XLA Modules:
  0.0 35.8 jit_solution(12324412579015691770)
XLA Ops:
  0.0 0.0 copy-start
  0.0 1.4 %copy-done = bf16[64,8,1536]{2,1,0:T(8,128)(2,1)S(1)} copy-done((bf16[64,8,1536]{2,1,0:T(8,128)(2,1)S(1)}, bf16[64,8,1536]{2,1,0:T(8,128)(2,1)}, u32[]{:S(2)}) %copy-start) | copy-done | bytes 1572888
  1.4 0.0 copy-start.3
  1.4 0.0 copy-start.4
  1.4 0.3 cross_rows.1
  1.8 0.3 pair_rows.1
  2.1 0.6 %collective-permute-start = (bf16[128,1536]{1,0:T(8,128)(2,1)S(1)}, bf16[128,1536]{1,0:T(8,128)(2,1)S(1)}, u32[]{:S(2)}, u32[]{:S(2)}) collective-permute-start(bf16[128,1536]{1,0:T(8,128)(2,1)S(1)} %pair_rows.1), channel_id=1, source_target_pairs={{0,4},{4,0},{8,12},{12,8},{16,20},{20,16},{24,28},{28,24},{1,5},{5... | collective-permute-start | bytes 1179656 | tf_op jit(solution)/shard_map/ppermute | solution.py:490
  2.7 3.5 %collective-permute-start.2 = (bf16[64,1536]{1,0:T(8,128)(2,1)S(1)}, bf16[64,1536]{1,0:T(8,128)(2,1)S(1)}, u32[]{:S(2)}, u32[]{:S(2)}) collective-permute-start(bf16[64,1536]{1,0:T(8,128)(2,1)S(1)} %get-tuple-element.18), channel_id=1, source_target_pairs={{0,28},{4,8},{8,4},{12,16},{16,12},{20,24},{24,20},{28,0},{1,29},{... | collective-permute-start | bytes 589832 | tf_op jit(solution)/shard_map/ppermute | solution.py:479
  6.2 0.0 collective-permute-start.1
  6.3 0.0 copy-done.3
  6.3 0.0 copy-done.4
  6.3 6.2 %interior.1 = (f32[4,64,1536]{2,1,0:T(8,128)S(1)}, bf16[1280,64]{1,0:T(8,128)(2,1)S(1)}, bf16[1536,256]{1,0:T(8,128)(2,1)S(1)}, bf16[8,12,16,128]{3,2,1,0:T(8,128)(2,1)S(1)}) custom-call(bf16[5,5,16,64]{3,2,1,0:T(8,128)(2,1)S(1)} %bitcast.7, f32[1,64]{1,0:T(1,128)S(1)} %bitcast.8, bf16[512,1536]{1,0:T(8,128)(2,1)S(1)} %get-tuple-element.12.refs_2_.refs_0_), custom_call_target="tpu_custom_call" | custom-call | flops 1006632960 | bytes 4540672 | tf_op jit(solution)/shard_map/interior/pallas_call | solution.py:49
  12.5 0.0 collective-permute-done.2.refs_3_
  12.5 0.0 collective-permute-done.refs_2_
  12.5 1.3 %rim_first.1.refs_6_ = bf16[4,32,1536]{2,1,0:T(8,128)(2,1)S(1)} custom-call(bf16[1280,64]{1,0:T(8,128)(2,1)S(1)} %get-tuple-element.13.refs_0_, f32[4,64,1536]{2,1,0:T(8,128)S(1)} %get-tuple-element.14.refs_1_, bf16[128,1536]{1,0:T(8,128)(2,1)S(1)} %collective-permute-done.refs_2_, bf16[64,1536]{1,0:T(8,128)(2,1)S(1)} %collective-permute-done.2.refs_3_), custom_call_target="tpu_custom_call" | custom-call | flops 125829120 | bytes 2719744 | tf_op jit(solution)/shard_map/rim_first/pallas_call | solution.py:49
  13.8 1.3 %collective-permute-done.1.refs_3_ = bf16[64,1536]{1,0:T(8,128)(2,1)S(1)} collective-permute-done((bf16[64,1536]{1,0:T(8,128)(2,1)S(1)}, bf16[64,1536]{1,0:T(8,128)(2,1)S(1)}, u32[]{:S(2)}, u32[]{:S(2)}) %collective-permute-start.1) | collective-permute-done | bytes 196640 | tf_op jit(solution)/shard_map/ppermute | solution.py:479
  15.1 0.0 copy-start.1
  15.1 0.0 copy-start.2
  15.1 2.4 %rim_last.1 = bf16[8,16,16,128]{3,2,1,0:T(8,128)(2,1)} custom-call(bf16[1280,64]{1,0:T(8,128)(2,1)S(1)} %get-tuple-element.13.refs_0_, f32[4,64,1536]{2,1,0:T(8,128)S(1)} %get-tuple-element.14.refs_1_, bf16[128,1536]{1,0:T(8,128)(2,1)S(1)} %collective-permute-done.refs_2_, bf16[64,1536]{1,0:T(8,128)(2,1)S(1)} %collective-permute-done.1.refs_3_, ...), custom_call_target="tpu_custom_call" | custom-call | flops 125829120 | bytes 4423680 | tf_op jit(solution)/shard_map/rim_last/pallas_call | solution.py:49
  17.5 4.2 %all-to-all-start = ((bf16[8,16,16,128]{3,2,1,0:T(8,128)(2,1)}), bf16[8,16,16,128]{3,2,1,0:T(8,128)(2,1)}, u32[]{:S(2)}, u32[]{:S(2)}) async-start(bf16[8,16,16,128]{3,2,1,0:T(8,128)(2,1)} %rim_last.1), calls=%async_computation | async-start | bytes 1048576 | tf_op jit(solution)/shard_map/all_to_all | solution.py:541
  21.8 0.0 copy-done.1
  21.8 0.0 copy-done.2
  21.8 3.2 %tables.1.refs_1_ = bf16[16,768,128]{2,1,0:T(8,128)(2,1)S(1)} custom-call(f32[4,16]{1,0:T(4,128)S(1)} %pad_maximum_fusion.refs_0_, f32[3,8,128]{2,1,0:T(8,128)S(1)} %copy-done.2, bf16[5,5,16,64]{3,2,1,0:T(8,128)(2,1)S(1)} %bitcast.6), custom_call_target="tpu_custom_call" | custom-call | flops 20971520 | bytes 3209472 | tf_op jit(solution)/shard_map/tables/pallas_call | solution.py:49
  25.0 6.4 %all-to-all-done.refs_0_ = bf16[8,16,16,128]{3,2,1,0:T(8,128)(2,1)} async-done(((bf16[8,16,16,128]{3,2,1,0:T(8,128)(2,1)}), bf16[8,16,16,128]{3,2,1,0:T(8,128)(2,1)}, u32[]{:S(2)}, u32[]{:S(2)}) %all-to-all-start) | async-done | bytes 524320 | tf_op jit(solution)/shard_map/all_to_all | solution.py:541
  31.4 4.4 %project.1 = f32[16,2,128,128]{3,2,1,0:T(8,128)} custom-call(bf16[8,16,16,128]{3,2,1,0:T(8,128)(2,1)} %all-to-all-done.refs_0_, bf16[16,768,128]{2,1,0:T(8,128)(2,1)S(1)} %tables.1.refs_1_), custom_call_target="tpu_custom_call" | custom-call | flops 268435456 | bytes 5767168 | tf_op jit(solution)/shard_map/project/pallas_call | solution.py:49
  (3 shorter events, 0.1 us)
Async XLA Ops:
  0.0 1.4 %copy-start = (bf16[64,8,1536]{2,1,0:T(8,128)(2,1)S(1)}, bf16[64,8,1536]{2,1,0:T(8,128)(2,1)}, u32[]{:S(2)}) copy-start(bf16[64,8,1536]{2,1,0:T(8,128)(2,1)} %param.5) | copy-start | bytes 4718596
  1.4 4.8 %copy-start.3 = (bf16[64,16,5,5]{0,1,3,2:T(8,128)(2,1)S(1)}, bf16[64,16,5,5]{0,1,3,2:T(8,128)(2,1)}, u32[]{:S(2)}) copy-start(bf16[64,16,5,5]{0,1,3,2:T(8,128)(2,1)} %param.6) | copy-start | bytes 153604
  1.4 4.8 %copy-start.4 = (f32[64]{0:T(128)S(1)}, f32[64]{0:T(128)}, u32[]{:S(2)}) copy-start(f32[64]{0:T(128)} %param.7) | copy-start | bytes 772
  2.1 10.4 %collective-permute-start = (bf16[128,1536]{1,0:T(8,128)(2,1)S(1)}, bf16[128,1536]{1,0:T(8,128)(2,1)S(1)}, u32[]{:S(2)}, u32[]{:S(2)}) collective-permute-start(bf16[128,1536]{1,0:T(8,128)(2,1)S(1)} %pair_rows.1), channel_id=1, source_target_pairs={{0,4},{4,0},{8,12},{12,8},{16,20},{20,16},{24,28},{28,24},{1,5},{5... | collective-permute-start | bytes 1179656 | tf_op jit(solution)/shard_map/ppermute | solution.py:490
  2.7 9.8 %collective-permute-start.2 = (bf16[64,1536]{1,0:T(8,128)(2,1)S(1)}, bf16[64,1536]{1,0:T(8,128)(2,1)S(1)}, u32[]{:S(2)}, u32[]{:S(2)}) collective-permute-start(bf16[64,1536]{1,0:T(8,128)(2,1)S(1)} %get-tuple-element.18), channel_id=1, source_target_pairs={{0,28},{4,8},{8,4},{12,16},{16,12},{20,24},{24,20},{28,0},{1,29},{... | collective-permute-start | bytes 589832 | tf_op jit(solution)/shard_map/ppermute | solution.py:479
  6.2 8.8 %collective-permute-start.1 = (bf16[64,1536]{1,0:T(8,128)(2,1)S(1)}, bf16[64,1536]{1,0:T(8,128)(2,1)S(1)}, u32[]{:S(2)}, u32[]{:S(2)}) collective-permute-start(bf16[64,1536]{1,0:T(8,128)(2,1)S(1)} %get-tuple-element.15), channel_id=1, source_target_pairs={{0,28},{4,8},{8,4},{12,16},{16,12},{20,24},{24,20},{28,0},{1,29},{... | collective-permute-start | bytes 589832 | tf_op jit(solution)/shard_map/ppermute | solution.py:479
  15.1 6.7 %copy-start.1 = (bf16[64,16,5,5]{0,1,3,2:T(8,128)(2,1)S(1)}, bf16[64,16,5,5]{0,1,3,2:T(8,128)(2,1)}, u32[]{:S(2)}) copy-start(bf16[64,16,5,5]{0,1,3,2:T(8,128)(2,1)} %param.8) | copy-start | bytes 153604
  15.1 6.7 %copy-start.2 = (f32[3,8,128]{2,1,0:T(8,128)S(1)}, f32[3,8,128]{2,1,0:T(8,128)}, u32[]{:S(2)}) copy-start(f32[3,8,128]{2,1,0:T(8,128)} %constant.17.clone.refs_1_) | copy-start | bytes 36868
  17.5 13.9 %all-to-all-start = ((bf16[8,16,16,128]{3,2,1,0:T(8,128)(2,1)}), bf16[8,16,16,128]{3,2,1,0:T(8,128)(2,1)}, u32[]{:S(2)}, u32[]{:S(2)}) async-start(bf16[8,16,16,128]{3,2,1,0:T(8,128)(2,1)} %rim_last.1), calls=%async_computation | async-start | bytes 1048576 | tf_op jit(solution)/shard_map/all_to_all | solution.py:541

commit v4 on v3

--- a/solution.py
+++ b/solution.py
@@ -122,11 +122,10 @@
 
 
 def cross_kernel(group, radius, groups, field_ref, kept_ref, *cross_refs):
-    share = groups // len(cross_refs)
     depth = radius * group
-    for g, rows in enumerate(picked(group, radius, groups, field_ref, 1)):
-        start = g % share * depth
-        cross_refs[g // share][start : start + depth, :] = rows
+    slots = [(ref, at) for ref in cross_refs for at in range(ref.shape[0] // depth)]
+    for (ref, at), rows in zip(slots, picked(group, radius, groups, field_ref, 1)):
+        ref[at * depth : (at + 1) * depth, :] = rows
     kept_ref[...] = field_ref[...]
 
 
@@ -463,13 +462,12 @@
     first_taps = first_weight.transpose(2, 3, 1, 0)
     second_taps = second_weight.transpose(2, 3, 1, 0)
     flat = atmosphere.reshape(channels * height, length)
-    shares = 2 if groups % 2 == 0 else 1
-    share = groups // shares
-    part = shapes((share * group * radius, length), BF16)
+    share = -(-groups // 4)
+    parts = [count for count in (groups - share, share) if count]
     flat, *crossed = call(
         lambda *refs: cross_kernel(group, radius, groups, *refs),
         "cross_rows",
-        (shapes(flat.shape, BF16),) + (part,) * shares,
+        (shapes(flat.shape, BF16),) + tuple(shapes((p * group * radius, length), BF16) for p in parts),
         [],
         6,
         2 * radius * channels * block * length,
@@ -513,9 +511,9 @@
     flops = 8 * rim_rows * radius * group * length * share
     before = [
         call(
-            lambda *refs: first_rim_kernel(group, radius, (0, share), *refs),
+            lambda *refs: first_rim_kernel(group, radius, (0, groups - share), *refs),
             "rim_first",
-            shapes((2 * radius, share * group, length), BF16),
+            shapes((2 * radius, (groups - share) * group, length), BF16),
             [partial],
             6,
             flops,

time: 36 us -> 35.7 us (level)
  waiting for transfers between devices: 7.67 us -> 7.2 us
    ppermute x2, waiting for transfers between devices: 1.27 us -> 0.67 us  [per_device(): crossed = [lax.ppermute(cross, 'lat', crosses) for cross in crossed]]
  transfers between devices with their start and end apart: 4 -> 4, of which waited for: 2 -> 2; matrix products, arithmetic and copies ran while one was open for 0% -> 0% of each run, Pallas kernels for 30% -> 32%
where the time goes in v4:
time: 35.7 us; the launch traced here: 35.4 us
  Pallas kernels  18.3 us (51%)
  starting transfers between devices  8.3 us (23%)
  waiting for transfers between devices  7.2 us (20%)
  local copies, waits for them, and re-layouts  1.42 us (4%)
    pallas_call x7, Pallas kernels, call(): pl.pallas_call(kernel, out_shape=out_shape, in_specs=in_specs or [VMEM] *...  18.3 us
    all_to_all x1, waiting for transfers between devices, per_device(): got = lax.all_to_all(send, 'lat', 0, 0, tiled=True)  6.53 us
    all_to_all x1, starting transfers between devices, per_device(): got = lax.all_to_all(send, 'lat', 0, 0, tiled=True)  4.16 us
    ppermute x2, starting transfers between devices, per_device(): crossed = [lax.ppermute(cross, 'lat', crosses) for cross in crossed]  3.58 us
    unnamed x10, local copies, waits for them, and re-layouts  1.42 us
  transfers between devices with their start and end apart: 4, of which 2 were waited for; matrix products, arithmetic and copies ran while one was open for 0% of the time, Pallas kernels for 32%

profile of v4, /device:TPU:0, one launch (start us, length us, event | category | flops | bytes accessed | tf_op | source)
XLA Modules:
  0.0 35.4 jit_solution(918143026667294939)
XLA Ops:
  0.0 0.0 copy-start
  0.0 1.4 %copy-done = bf16[64,8,1536]{2,1,0:T(8,128)(2,1)S(1)} copy-done((bf16[64,8,1536]{2,1,0:T(8,128)(2,1)S(1)}, bf16[64,8,1536]{2,1,0:T(8,128)(2,1)}, u32[]{:S(2)}) %copy-start) | copy-done | bytes 1572888
  1.4 0.0 copy-start.3
  1.4 0.0 copy-start.4
  1.4 0.3 cross_rows.1
  1.8 0.3 pair_rows.1
  2.1 0.6 %collective-permute-start = (bf16[128,1536]{1,0:T(8,128)(2,1)S(1)}, bf16[128,1536]{1,0:T(8,128)(2,1)S(1)}, u32[]{:S(2)}, u32[]{:S(2)}) collective-permute-start(bf16[128,1536]{1,0:T(8,128)(2,1)S(1)} %pair_rows.1), channel_id=1, source_target_pairs={{0,4},{4,0},{8,12},{12,8},{16,20},{20,16},{24,28},{28,24},{1,5},{5... | collective-permute-start | bytes 1179656 | tf_op jit(solution)/shard_map/ppermute | solution.py:488
  2.7 3.5 %collective-permute-start.2 = (bf16[96,1536]{1,0:T(8,128)(2,1)S(1)}, bf16[96,1536]{1,0:T(8,128)(2,1)S(1)}, u32[]{:S(2)}, u32[]{:S(2)}) collective-permute-start(bf16[96,1536]{1,0:T(8,128)(2,1)S(1)} %get-tuple-element.18), channel_id=1, source_target_pairs={{0,28},{4,8},{8,4},{12,16},{16,12},{20,24},{24,20},{28,0},{1,29},{... | collective-permute-start | bytes 884744 | tf_op jit(solution)/shard_map/ppermute | solution.py:477
  6.2 0.0 collective-permute-start.1
  6.3 0.0 copy-done.3
  6.3 0.0 copy-done.4
  6.3 6.2 %interior.1 = (f32[4,64,1536]{2,1,0:T(8,128)S(1)}, bf16[1280,64]{1,0:T(8,128)(2,1)S(1)}, bf16[1536,256]{1,0:T(8,128)(2,1)S(1)}, bf16[8,12,16,128]{3,2,1,0:T(8,128)(2,1)S(1)}) custom-call(bf16[5,5,16,64]{3,2,1,0:T(8,128)(2,1)S(1)} %bitcast.7, f32[1,64]{1,0:T(1,128)S(1)} %bitcast.8, bf16[512,1536]{1,0:T(8,128)(2,1)S(1)} %get-tuple-element.12.refs_2_.refs_0_), custom_call_target="tpu_custom_call" | custom-call | flops 1006632960 | bytes 4540672 | tf_op jit(solution)/shard_map/interior/pallas_call | solution.py:49
  12.5 0.6 %collective-permute-done.2.refs_3_ = bf16[96,1536]{1,0:T(8,128)(2,1)S(1)} collective-permute-done((bf16[96,1536]{1,0:T(8,128)(2,1)S(1)}, bf16[96,1536]{1,0:T(8,128)(2,1)S(1)}, u32[]{:S(2)}, u32[]{:S(2)}) %collective-permute-start.2) | collective-permute-done | bytes 294944 | tf_op jit(solution)/shard_map/ppermute | solution.py:477
  13.1 0.0 collective-permute-done.refs_2_
  13.1 1.9 %rim_first.1.refs_6_ = bf16[4,48,1536]{2,1,0:T(8,128)(2,1)S(1)} custom-call(bf16[1280,64]{1,0:T(8,128)(2,1)S(1)} %get-tuple-element.13.refs_0_, f32[4,64,1536]{2,1,0:T(8,128)S(1)} %get-tuple-element.14.refs_1_, bf16[128,1536]{1,0:T(8,128)(2,1)S(1)} %collective-permute-done.refs_2_, bf16[96,1536]{1,0:T(8,128)(2,1)S(1)} %collective-permute-done.2.refs_3_), custom_call_target="tpu_custom_call" | custom-call | flops 62914560 | bytes 3014656 | tf_op jit(solution)/shard_map/rim_first/pallas_call | solution.py:49
  15.0 0.0 collective-permute-done.1.refs_3_
  15.1 0.0 copy-start.1
  15.1 0.0 copy-start.2
  15.1 1.9 %rim_last.1 = bf16[8,16,16,128]{3,2,1,0:T(8,128)(2,1)} custom-call(bf16[1280,64]{1,0:T(8,128)(2,1)S(1)} %get-tuple-element.13.refs_0_, f32[4,64,1536]{2,1,0:T(8,128)S(1)} %get-tuple-element.14.refs_1_, bf16[128,1536]{1,0:T(8,128)(2,1)S(1)} %collective-permute-done.refs_2_, bf16[32,1536]{1,0:T(8,128)(2,1)S(1)} %collective-permute-done.1.refs_3_, ...), custom_call_target="tpu_custom_call" | custom-call | flops 62914560 | bytes 4521984 | tf_op jit(solution)/shard_map/rim_last/pallas_call | solution.py:49
  17.0 4.2 %all-to-all-start = ((bf16[8,16,16,128]{3,2,1,0:T(8,128)(2,1)}), bf16[8,16,16,128]{3,2,1,0:T(8,128)(2,1)}, u32[]{:S(2)}, u32[]{:S(2)}) async-start(bf16[8,16,16,128]{3,2,1,0:T(8,128)(2,1)} %rim_last.1), calls=%async_computation | async-start | bytes 1048576 | tf_op jit(solution)/shard_map/all_to_all | solution.py:539
  21.3 0.0 copy-done.1
  21.3 0.0 copy-done.2
  21.3 3.2 %tables.1.refs_1_ = bf16[16,768,128]{2,1,0:T(8,128)(2,1)S(1)} custom-call(f32[4,16]{1,0:T(4,128)S(1)} %pad_maximum_fusion.refs_0_, f32[3,8,128]{2,1,0:T(8,128)S(1)} %copy-done.2, bf16[5,5,16,64]{3,2,1,0:T(8,128)(2,1)S(1)} %bitcast.6), custom_call_target="tpu_custom_call" | custom-call | flops 20971520 | bytes 3209472 | tf_op jit(solution)/shard_map/tables/pallas_call | solution.py:49
  24.5 6.5 %all-to-all-done.refs_0_ = bf16[8,16,16,128]{3,2,1,0:T(8,128)(2,1)} async-done(((bf16[8,16,16,128]{3,2,1,0:T(8,128)(2,1)}), bf16[8,16,16,128]{3,2,1,0:T(8,128)(2,1)}, u32[]{:S(2)}, u32[]{:S(2)}) %all-to-all-start) | async-done | bytes 524320 | tf_op jit(solution)/shard_map/all_to_all | solution.py:539
  31.0 4.4 %project.1 = f32[16,2,128,128]{3,2,1,0:T(8,128)} custom-call(bf16[8,16,16,128]{3,2,1,0:T(8,128)(2,1)} %all-to-all-done.refs_0_, bf16[16,768,128]{2,1,0:T(8,128)(2,1)S(1)} %tables.1.refs_1_), custom_call_target="tpu_custom_call" | custom-call | flops 268435456 | bytes 5767168 | tf_op jit(solution)/shard_map/project/pallas_call | solution.py:49
  (3 shorter events, 0.1 us)
Async XLA Ops:
  0.0 1.4 %copy-start = (bf16[64,8,1536]{2,1,0:T(8,128)(2,1)S(1)}, bf16[64,8,1536]{2,1,0:T(8,128)(2,1)}, u32[]{:S(2)}) copy-start(bf16[64,8,1536]{2,1,0:T(8,128)(2,1)} %param.5) | copy-start | bytes 4718596
  1.4 4.8 %copy-start.3 = (bf16[64,16,5,5]{0,1,3,2:T(8,128)(2,1)S(1)}, bf16[64,16,5,5]{0,1,3,2:T(8,128)(2,1)}, u32[]{:S(2)}) copy-start(bf16[64,16,5,5]{0,1,3,2:T(8,128)(2,1)} %param.6) | copy-start | bytes 153604
  1.4 4.8 %copy-start.4 = (f32[64]{0:T(128)S(1)}, f32[64]{0:T(128)}, u32[]{:S(2)}) copy-start(f32[64]{0:T(128)} %param.7) | copy-start | bytes 772
  2.1 11.0 %collective-permute-start = (bf16[128,1536]{1,0:T(8,128)(2,1)S(1)}, bf16[128,1536]{1,0:T(8,128)(2,1)S(1)}, u32[]{:S(2)}, u32[]{:S(2)}) collective-permute-start(bf16[128,1536]{1,0:T(8,128)(2,1)S(1)} %pair_rows.1), channel_id=1, source_target_pairs={{0,4},{4,0},{8,12},{12,8},{16,20},{20,16},{24,28},{28,24},{1,5},{5... | collective-permute-start | bytes 1179656 | tf_op jit(solution)/shard_map/ppermute | solution.py:488
  2.7 10.4 %collective-permute-start.2 = (bf16[96,1536]{1,0:T(8,128)(2,1)S(1)}, bf16[96,1536]{1,0:T(8,128)(2,1)S(1)}, u32[]{:S(2)}, u32[]{:S(2)}) collective-permute-start(bf16[96,1536]{1,0:T(8,128)(2,1)S(1)} %get-tuple-element.18), channel_id=1, source_target_pairs={{0,28},{4,8},{8,4},{12,16},{16,12},{20,24},{24,20},{28,0},{1,29},{... | collective-permute-start | bytes 884744 | tf_op jit(solution)/shard_map/ppermute | solution.py:477
  6.2 8.8 %collective-permute-start.1 = (bf16[32,1536]{1,0:T(8,128)(2,1)S(1)}, bf16[32,1536]{1,0:T(8,128)(2,1)S(1)}, u32[]{:S(2)}, u32[]{:S(2)}) collective-permute-start(bf16[32,1536]{1,0:T(8,128)(2,1)S(1)} %get-tuple-element.15), channel_id=1, source_target_pairs={{0,28},{4,8},{8,4},{12,16},{16,12},{20,24},{24,20},{28,0},{1,29},{... | collective-permute-start | bytes 294920 | tf_op jit(solution)/shard_map/ppermute | solution.py:477
  15.1 6.2 %copy-start.1 = (bf16[64,16,5,5]{0,1,3,2:T(8,128)(2,1)S(1)}, bf16[64,16,5,5]{0,1,3,2:T(8,128)(2,1)}, u32[]{:S(2)}) copy-start(bf16[64,16,5,5]{0,1,3,2:T(8,128)(2,1)} %param.8) | copy-start | bytes 153604
  15.1 6.2 %copy-start.2 = (f32[3,8,128]{2,1,0:T(8,128)S(1)}, f32[3,8,128]{2,1,0:T(8,128)}, u32[]{:S(2)}) copy-start(f32[3,8,128]{2,1,0:T(8,128)} %constant.17.clone.refs_1_) | copy-start | bytes 36868
  17.0 14.0 %all-to-all-start = ((bf16[8,16,16,128]{3,2,1,0:T(8,128)(2,1)}), bf16[8,16,16,128]{3,2,1,0:T(8,128)(2,1)}, u32[]{:S(2)}, u32[]{:S(2)}) async-start(bf16[8,16,16,128]{3,2,1,0:T(8,128)(2,1)} %rim_last.1), calls=%async_computation | async-start | bytes 1048576 | tf_op jit(solution)/shard_map/all_to_all | solution.py:539

commit v5 on v4

--- a/solution.py
+++ b/solution.py
@@ -19,10 +19,6 @@
     return lax.dot_general(left, right, (((0,), (0,)), ((), ())), preferred_element_type=F32)
 
 
-def dot_nt(left, right):
-    return lax.dot_general(left, right, (((1,), (1,)), ((), ())), preferred_element_type=F32)
-
-
 def dot_nn(left, right):
     return jnp.dot(left, right, preferred_element_type=F32)
 
@@ -44,7 +40,7 @@
     return sum(math.prod(a.shape) * a.dtype.itemsize for a in jax.tree.leaves(arrays))
 
 
-def call(kernel, name, out_shape, scratch, mebibytes, flops, args, in_specs=None, out_specs=None):
+def call(kernel, out_shape, scratch, mebibytes, flops, args, in_specs=None, out_specs=None):
     size = bytes_of((args, out_shape))
     return pl.pallas_call(
         kernel,
@@ -54,7 +50,6 @@
         scratch_shapes=scratch,
         compiler_params=pltpu.CompilerParams(vmem_limit_bytes=mebibytes * 2**20),
         cost_estimate=pl.CostEstimate(flops=flops, transcendentals=0, bytes_accessed=size),
-        name=name,
     )(*args)
 
 
@@ -466,7 +461,6 @@
     parts = [count for count in (groups - share, share) if count]
     flat, *crossed = call(
         lambda *refs: cross_kernel(group, radius, groups, *refs),
-        "cross_rows",
         (shapes(flat.shape, BF16),) + tuple(shapes((p * group * radius, length), BF16) for p in parts),
         [],
         6,
@@ -474,10 +468,10 @@
         (flat,),
     )
     crosses = [(i, (i + 1 if i % 2 else i - 1) % members) for i in range(members)]
-    crossed = [lax.ppermute(cross, "lat", crosses) for cross in crossed]
+    for at, cross in enumerate(crossed):
+        crossed[at] = lax.ppermute(cross, "lat", crosses)
     pair = call(
         lambda *refs: pair_kernel(group, radius, groups, *refs),
-        "pair_rows",
         shapes((channels * radius, length), BF16),
         [],
         6,
@@ -489,7 +483,6 @@
 
     edge, rim, fourier, early = call(
         lambda *refs: interior_kernel(group, *refs),
-        "interior",
         (
             shapes((2 * radius, channels, length), F32),
             shapes((groups * 2 * rim_rows, 2 * radius * group), BF16),
@@ -512,7 +505,6 @@
     before = [
         call(
             lambda *refs: first_rim_kernel(group, radius, (0, groups - share), *refs),
-            "rim_first",
             shapes((2 * radius, (groups - share) * group, length), BF16),
             [partial],
             6,
@@ -523,7 +515,6 @@
     ]
     send = call(
         lambda *refs: last_rim_kernel(group, radius, (groups - share, groups), *refs),
-        "rim_last",
         shapes((members, 2 * height, owned, wide), BF16),
         [
             partial,
@@ -549,7 +540,6 @@
     sphere = np.repeat(sphere.reshape(3, head, LANES // owned), owned, axis=2)
     table = call(
         lambda *refs: tables_kernel(group, *refs),
-        "tables",
         shapes((owned, taps * wide + 2 * places, max(wide, DEGREES // 2)), BF16),
         [
             pltpu.VMEM((DEGREES * head, LANES), F32),
@@ -566,7 +556,6 @@
     lanes = max(wide, LANES)
     spectrum = call(
         lambda *refs: project_kernel(radius, *refs),
-        "project",
         shapes((owned, 2, wide, DEGREES // 2), F32),
         [
             pltpu.VMEM(((places + 2 * radius) * (owned + 1), lanes), F32),
@@ -589,6 +578,7 @@
         P("chan"),
         P("chan", None, None, None),
     )
+
     return jax.shard_map(
         per_device,
         mesh=mesh,

time: 35.7 us -> 35.7 us (level)
  no operation moved by 1% of the time
where the time goes in v5:
time: 35.7 us; the launch traced here: 35.4 us
  Pallas kernels  18.3 us (51%)
  starting transfers between devices  8.3 us (23%)
  waiting for transfers between devices  7.2 us (20%)
  local copies, waits for them, and re-layouts  1.42 us (4%)
    pallas_call x7, Pallas kernels, call(): pl.pallas_call(kernel, out_shape=out_shape, in_specs=in_specs or [VMEM] *...  18.3 us
    all_to_all x1, waiting for transfers between devices, per_device(): got = lax.all_to_all(send, 'lat', 0, 0, tiled=True)  6.53 us
    all_to_all x1, starting transfers between devices, per_device(): got = lax.all_to_all(send, 'lat', 0, 0, tiled=True)  4.16 us
    ppermute x2, starting transfers between devices, per_device(): crossed[at] = lax.ppermute(cross, 'lat', crosses)  3.58 us
    unnamed x10, local copies, waits for them, and re-layouts  1.42 us
  transfers between devices with their start and end apart: 4, of which 2 were waited for; matrix products, arithmetic and copies ran while one was open for 0% of the time, Pallas kernels for 32%

profile of v5, /device:TPU:0, one launch (start us, length us, event | category | flops | bytes accessed | tf_op | source)
XLA Modules:
  0.0 35.4 jit_solution(918143026667294939)
XLA Ops:
  0.0 0.0 copy-start
  0.0 1.4 %copy-done = bf16[64,8,1536]{2,1,0:T(8,128)(2,1)S(1)} copy-done((bf16[64,8,1536]{2,1,0:T(8,128)(2,1)S(1)}, bf16[64,8,1536]{2,1,0:T(8,128)(2,1)}, u32[]{:S(2)}) %copy-start) | copy-done | bytes 1572888
  1.4 0.0 copy-start.3
  1.4 0.0 copy-start.4
  1.4 0.3 shard_map.55
  1.8 0.3 shard_map.57
  2.1 0.6 %collective-permute-start = (bf16[128,1536]{1,0:T(8,128)(2,1)S(1)}, bf16[128,1536]{1,0:T(8,128)(2,1)S(1)}, u32[]{:S(2)}, u32[]{:S(2)}) collective-permute-start(bf16[128,1536]{1,0:T(8,128)(2,1)S(1)} %shard_map.57), channel_id=1, source_target_pairs={{0,4},{4,0},{8,12},{12,8},{16,20},{20,16},{24,28},{28,24},{1,5},{5... | collective-permute-start | bytes 1179656 | tf_op jit(solution)/shard_map/ppermute | solution.py:482
  2.7 3.5 %collective-permute-start.2 = (bf16[96,1536]{1,0:T(8,128)(2,1)S(1)}, bf16[96,1536]{1,0:T(8,128)(2,1)S(1)}, u32[]{:S(2)}, u32[]{:S(2)}) collective-permute-start(bf16[96,1536]{1,0:T(8,128)(2,1)S(1)} %get-tuple-element.18), channel_id=1, source_target_pairs={{0,28},{4,8},{8,4},{12,16},{16,12},{20,24},{24,20},{28,0},{1,29},{... | collective-permute-start | bytes 884744 | tf_op jit(solution)/shard_map/ppermute | solution.py:472
  6.2 0.0 collective-permute-start.1
  6.3 0.0 copy-done.3
  6.3 0.0 copy-done.4
  6.3 6.2 %shard_map.56 = (f32[4,64,1536]{2,1,0:T(8,128)S(1)}, bf16[1280,64]{1,0:T(8,128)(2,1)S(1)}, bf16[1536,256]{1,0:T(8,128)(2,1)S(1)}, bf16[8,12,16,128]{3,2,1,0:T(8,128)(2,1)S(1)}) custom-call(bf16[5,5,16,64]{3,2,1,0:T(8,128)(2,1)S(1)} %bitcast.7, f32[1,64]{1,0:T(1,128)S(1)} %bitcast.8, bf16[512,1536]{1,0:T(8,128)(2,1)S(1)} %get-tuple-element.12.refs_2_.refs_0_), custom_call_target="tpu_custom_call" | custom-call | flops 1006632960 | bytes 4540672 | tf_op jit(solution)/shard_map/pallas_call | solution.py:45
  12.5 0.6 %collective-permute-done.2.refs_3_ = bf16[96,1536]{1,0:T(8,128)(2,1)S(1)} collective-permute-done((bf16[96,1536]{1,0:T(8,128)(2,1)S(1)}, bf16[96,1536]{1,0:T(8,128)(2,1)S(1)}, u32[]{:S(2)}, u32[]{:S(2)}) %collective-permute-start.2) | collective-permute-done | bytes 294944 | tf_op jit(solution)/shard_map/ppermute | solution.py:472
  13.1 0.0 collective-permute-done.refs_2_
  13.1 1.9 %shard_map.58.refs_6_ = bf16[4,48,1536]{2,1,0:T(8,128)(2,1)S(1)} custom-call(bf16[1280,64]{1,0:T(8,128)(2,1)S(1)} %get-tuple-element.13.refs_0_, f32[4,64,1536]{2,1,0:T(8,128)S(1)} %get-tuple-element.14.refs_1_, bf16[128,1536]{1,0:T(8,128)(2,1)S(1)} %collective-permute-done.refs_2_, bf16[96,1536]{1,0:T(8,128)(2,1)S(1)} %collective-permute-done.2.refs_3_), custom_call_target="tpu_custom_call" | custom-call | flops 62914560 | bytes 3014656 | tf_op jit(solution)/shard_map/pallas_call | solution.py:45
  15.0 0.0 collective-permute-done.1.refs_3_
  15.1 0.0 copy-start.1
  15.1 0.0 copy-start.2
  15.1 1.9 %shard_map.59 = bf16[8,16,16,128]{3,2,1,0:T(8,128)(2,1)} custom-call(bf16[1280,64]{1,0:T(8,128)(2,1)S(1)} %get-tuple-element.13.refs_0_, f32[4,64,1536]{2,1,0:T(8,128)S(1)} %get-tuple-element.14.refs_1_, bf16[128,1536]{1,0:T(8,128)(2,1)S(1)} %collective-permute-done.refs_2_, bf16[32,1536]{1,0:T(8,128)(2,1)S(1)} %collective-permute-done.1.refs_3_, ...), custom_call_target="tpu_custom_call" | custom-call | flops 62914560 | bytes 4521984 | tf_op jit(solution)/shard_map/pallas_call | solution.py:45
  17.0 4.2 %all-to-all-start = ((bf16[8,16,16,128]{3,2,1,0:T(8,128)(2,1)}), bf16[8,16,16,128]{3,2,1,0:T(8,128)(2,1)}, u32[]{:S(2)}, u32[]{:S(2)}) async-start(bf16[8,16,16,128]{3,2,1,0:T(8,128)(2,1)} %shard_map.59), calls=%async_computation | async-start | bytes 1048576 | tf_op jit(solution)/shard_map/all_to_all | solution.py:530
  21.3 0.0 copy-done.1
  21.3 0.0 copy-done.2
  21.3 3.2 %shard_map.60.refs_1_ = bf16[16,768,128]{2,1,0:T(8,128)(2,1)S(1)} custom-call(f32[4,16]{1,0:T(4,128)S(1)} %pad_maximum_fusion.refs_0_, f32[3,8,128]{2,1,0:T(8,128)S(1)} %copy-done.2, bf16[5,5,16,64]{3,2,1,0:T(8,128)(2,1)S(1)} %bitcast.6), custom_call_target="tpu_custom_call" | custom-call | flops 20971520 | bytes 3209472 | tf_op jit(solution)/shard_map/pallas_call | solution.py:45
  24.5 6.5 %all-to-all-done.refs_0_ = bf16[8,16,16,128]{3,2,1,0:T(8,128)(2,1)} async-done(((bf16[8,16,16,128]{3,2,1,0:T(8,128)(2,1)}), bf16[8,16,16,128]{3,2,1,0:T(8,128)(2,1)}, u32[]{:S(2)}, u32[]{:S(2)}) %all-to-all-start) | async-done | bytes 524320 | tf_op jit(solution)/shard_map/all_to_all | solution.py:530
  31.0 4.4 %shard_map.61 = f32[16,2,128,128]{3,2,1,0:T(8,128)} custom-call(bf16[8,16,16,128]{3,2,1,0:T(8,128)(2,1)} %all-to-all-done.refs_0_, bf16[16,768,128]{2,1,0:T(8,128)(2,1)S(1)} %shard_map.60.refs_1_), custom_call_target="tpu_custom_call" | custom-call | flops 268435456 | bytes 5767168 | tf_op jit(solution)/shard_map/pallas_call | solution.py:45
  (3 shorter events, 0.1 us)
Async XLA Ops:
  0.0 1.4 %copy-start = (bf16[64,8,1536]{2,1,0:T(8,128)(2,1)S(1)}, bf16[64,8,1536]{2,1,0:T(8,128)(2,1)}, u32[]{:S(2)}) copy-start(bf16[64,8,1536]{2,1,0:T(8,128)(2,1)} %param.5) | copy-start | bytes 4718596
  1.4 4.8 %copy-start.3 = (bf16[64,16,5,5]{0,1,3,2:T(8,128)(2,1)S(1)}, bf16[64,16,5,5]{0,1,3,2:T(8,128)(2,1)}, u32[]{:S(2)}) copy-start(bf16[64,16,5,5]{0,1,3,2:T(8,128)(2,1)} %param.6) | copy-start | bytes 153604
  1.4 4.8 %copy-start.4 = (f32[64]{0:T(128)S(1)}, f32[64]{0:T(128)}, u32[]{:S(2)}) copy-start(f32[64]{0:T(128)} %param.7) | copy-start | bytes 772
  2.1 11.0 %collective-permute-start = (bf16[128,1536]{1,0:T(8,128)(2,1)S(1)}, bf16[128,1536]{1,0:T(8,128)(2,1)S(1)}, u32[]{:S(2)}, u32[]{:S(2)}) collective-permute-start(bf16[128,1536]{1,0:T(8,128)(2,1)S(1)} %shard_map.57), channel_id=1, source_target_pairs={{0,4},{4,0},{8,12},{12,8},{16,20},{20,16},{24,28},{28,24},{1,5},{5... | collective-permute-start | bytes 1179656 | tf_op jit(solution)/shard_map/ppermute | solution.py:482
  2.7 10.4 %collective-permute-start.2 = (bf16[96,1536]{1,0:T(8,128)(2,1)S(1)}, bf16[96,1536]{1,0:T(8,128)(2,1)S(1)}, u32[]{:S(2)}, u32[]{:S(2)}) collective-permute-start(bf16[96,1536]{1,0:T(8,128)(2,1)S(1)} %get-tuple-element.18), channel_id=1, source_target_pairs={{0,28},{4,8},{8,4},{12,16},{16,12},{20,24},{24,20},{28,0},{1,29},{... | collective-permute-start | bytes 884744 | tf_op jit(solution)/shard_map/ppermute | solution.py:472
  6.2 8.8 %collective-permute-start.1 = (bf16[32,1536]{1,0:T(8,128)(2,1)S(1)}, bf16[32,1536]{1,0:T(8,128)(2,1)S(1)}, u32[]{:S(2)}, u32[]{:S(2)}) collective-permute-start(bf16[32,1536]{1,0:T(8,128)(2,1)S(1)} %get-tuple-element.15), channel_id=1, source_target_pairs={{0,28},{4,8},{8,4},{12,16},{16,12},{20,24},{24,20},{28,0},{1,29},{... | collective-permute-start | bytes 294920 | tf_op jit(solution)/shard_map/ppermute | solution.py:472
  15.1 6.2 %copy-start.1 = (bf16[64,16,5,5]{0,1,3,2:T(8,128)(2,1)S(1)}, bf16[64,16,5,5]{0,1,3,2:T(8,128)(2,1)}, u32[]{:S(2)}) copy-start(bf16[64,16,5,5]{0,1,3,2:T(8,128)(2,1)} %param.8) | copy-start | bytes 153604
  15.1 6.2 %copy-start.2 = (f32[3,8,128]{2,1,0:T(8,128)S(1)}, f32[3,8,128]{2,1,0:T(8,128)}, u32[]{:S(2)}) copy-start(f32[3,8,128]{2,1,0:T(8,128)} %constant.17.clone.refs_1_) | copy-start | bytes 36868
  17.0 14.0 %all-to-all-start = ((bf16[8,16,16,128]{3,2,1,0:T(8,128)(2,1)}), bf16[8,16,16,128]{3,2,1,0:T(8,128)(2,1)}, u32[]{:S(2)}, u32[]{:S(2)}) async-start(bf16[8,16,16,128]{3,2,1,0:T(8,128)(2,1)} %shard_map.59), calls=%async_computation | async-start | bytes 1048576 | tf_op jit(solution)/shard_map/all_to_all | solution.py:530

commit v6 on v5

--- a/solution.py
+++ b/solution.py
@@ -203,7 +203,7 @@
 
     lax.fori_loop(0, groups, per_group, 0)
 
-    found = dot_nn(field_ref[...], fourier_ref[...])
+    found = dot_nn(jnp.concatenate([field_ref[...], hidden_ref[...]], axis=0), fourier_ref[...])
     pitch = height + 1
     total = pitch * channels
     for part in range(2):
@@ -217,9 +217,9 @@
             spectra_ref[pl.ds(part * total + row, channels, stride=pitch), :] for part in range(2)
         )
         write_spectra(send_ref, row, real, imaginary)
-    found = dot_nn(hidden_ref[...], fourier_ref[...])
     for row in range(inner):
-        mine = found[row * channels : (row + 1) * channels, :]
+        start = (height + row) * channels
+        mine = found[start : start + channels, :]
         write_spectra(send_ref, height + row, mine[:, :orders], mine[:, orders:])
 
 
@@ -323,12 +323,12 @@
     cosine, log_sine, quadrature = sphere_ref[0], sphere_ref[1], sphere_ref[2]
     diagonal = jnp.exp(0.5 * (jnp.log((2.0 * order + 1.0) / 2.0) + log_ratio) + order * log_sine)
 
-    twice = (iota((channels, wide), 1) // 2 == iota((channels, wide), 0)).astype(F32).astype(BF16)
+    twice = (iota((channels, wide), 1) % channels == iota((channels, wide), 0)).astype(F32).astype(BF16)
     across = (iota((group, wide), 1) % group == iota((group, wide), 0)).astype(F32).astype(BF16)
     shape = (wide, wide)
     row, column = iota(shape, 0), iota(shape, 1)
-    row_part, column_part = row // channels, column % 2
-    same_group = row % channels // group == column // 2 // group
+    row_part, column_part = row // channels, column // channels
+    same_group = row % channels // group == column % channels // group
     straight = row_part == column_part
     sign = jnp.where(column_part > row_part, 1.0, -1.0)
     flat = jnp.concatenate([weight_ref[dy, dx] for dy in range(taps) for dx in range(taps)], axis=0)
@@ -405,18 +405,15 @@
                 place = height + row
             rows_ref[pad + start : pad + start + owned, :wide] = got_ref[source, place].astype(F32)
 
-    row, column = iota((wide, wide), 0), iota((wide, wide), 1)
-    identity = (row == column % 2 * (wide // 2) + column // 2).astype(F32).astype(BF16)
-    identity = jnp.concatenate([identity] * (2 if owned % 2 == 0 else 1), axis=1)
     mix = taps * wide
     half = out_ref.shape[3]
+    channels = wide // 2
 
     def sent(k):
         return pltpu.make_async_copy(out_ref.at[k], out_hbm.at[k], semaphores.at[k])
 
     def gathered(k):
         pieces = [rows_ref[pl.ds(dy * pitch + k, places, stride=pitch), :] for dy in range(taps)]
-        pieces.append(plain_ref[pl.ds(k, places, stride=pitch), :])
         return jnp.concatenate([piece[:, :wide].astype(BF16) for piece in pieces], axis=1)
 
     together = 2 if owned % 2 == 0 else 1
@@ -424,16 +421,19 @@
         orders = range(first, first + together)
         stacked = jnp.concatenate([gathered(k) for k in orders], axis=0)
         mixing = jnp.concatenate([table_ref[k, :mix, :wide] for k in orders], axis=1)
-        mixing = jnp.concatenate([mixing, identity], axis=0)
         both = dot_nn(stacked, mixing)
         for at, k in enumerate(orders):
-            mixed = both[at * places : (at + 1) * places, at * wide : (at + 1) * wide].T.astype(BF16)
+            mixed = both[at * places : (at + 1) * places, at * wide : (at + 1) * wide]
+            mixed = (mixed + plain_ref[pl.ds(k, places, stride=pitch), :][:, :wide]).T.astype(BF16)
             legendre = jnp.concatenate(
                 [table_ref[k, mix + q * places : mix + (q + 1) * places, :half] for q in range(2)], axis=1
             )
             found = dot_nn(mixed, legendre)
-            out_ref[k, 0] = found[:, :half]
-            out_ref[k, 1] = found[:, half:]
+            for part in range(2):
+                rows = pl.ds(part, channels, stride=2)
+                mine = found[part * channels : (part + 1) * channels, :]
+                out_ref[k, 0, rows, :] = mine[:, :half]
+                out_ref[k, 1, rows, :] = mine[:, half:]
             sent(k).start()
     for k in range(owned):
         sent(k).wait()

time: 35.7 us -> 35.5 us (level)
  no operation moved by 1% of the time
where the time goes in v6:
time: 35.5 us; the launch traced here: 35.3 us
  Pallas kernels  18.1 us (51%)
  starting transfers between devices  8.3 us (23%)
  waiting for transfers between devices  7.25 us (20%)
  local copies, waits for them, and re-layouts  1.42 us (4%)
    pallas_call x7, Pallas kernels, call(): pl.pallas_call(kernel, out_shape=out_shape, in_specs=in_specs or [VMEM] *...  18.1 us
    all_to_all x1, waiting for transfers between devices, per_device(): got = lax.all_to_all(send, 'lat', 0, 0, tiled=True)  6.53 us
    all_to_all x1, starting transfers between devices, per_device(): got = lax.all_to_all(send, 'lat', 0, 0, tiled=True)  4.16 us
    ppermute x2, starting transfers between devices, per_device(): crossed[at] = lax.ppermute(cross, 'lat', crosses)  3.58 us
    unnamed x10, local copies, waits for them, and re-layouts  1.42 us
    ppermute x2, waiting for transfers between devices, per_device(): crossed[at] = lax.ppermute(cross, 'lat', crosses)  0.72 us
  transfers between devices with their start and end apart: 4, of which 2 were waited for; matrix products, arithmetic and copies ran while one was open for 0% of the time, Pallas kernels for 32%

profile of v6, /device:TPU:0, one launch (start us, length us, event | category | flops | bytes accessed | tf_op | source)
XLA Modules:
  0.0 35.3 jit_solution(6687677182146742635)
XLA Ops:
  0.0 0.0 copy-start
  0.0 1.4 %copy-done = bf16[64,8,1536]{2,1,0:T(8,128)(2,1)S(1)} copy-done((bf16[64,8,1536]{2,1,0:T(8,128)(2,1)S(1)}, bf16[64,8,1536]{2,1,0:T(8,128)(2,1)}, u32[]{:S(2)}) %copy-start) | copy-done | bytes 1572888
  1.4 0.0 copy-start.3
  1.4 0.0 copy-start.4
  1.4 0.3 shard_map.55
  1.8 0.3 shard_map.57
  2.1 0.6 %collective-permute-start = (bf16[128,1536]{1,0:T(8,128)(2,1)S(1)}, bf16[128,1536]{1,0:T(8,128)(2,1)S(1)}, u32[]{:S(2)}, u32[]{:S(2)}) collective-permute-start(bf16[128,1536]{1,0:T(8,128)(2,1)S(1)} %shard_map.57), channel_id=1, source_target_pairs={{0,4},{4,0},{8,12},{12,8},{16,20},{20,16},{24,28},{28,24},{1,5},{5... | collective-permute-start | bytes 1179656 | tf_op jit(solution)/shard_map/ppermute | solution.py:482
  2.7 3.5 %collective-permute-start.2 = (bf16[96,1536]{1,0:T(8,128)(2,1)S(1)}, bf16[96,1536]{1,0:T(8,128)(2,1)S(1)}, u32[]{:S(2)}, u32[]{:S(2)}) collective-permute-start(bf16[96,1536]{1,0:T(8,128)(2,1)S(1)} %get-tuple-element.18), channel_id=1, source_target_pairs={{0,28},{4,8},{8,4},{12,16},{16,12},{20,24},{24,20},{28,0},{1,29},{... | collective-permute-start | bytes 884744 | tf_op jit(solution)/shard_map/ppermute | solution.py:472
  6.2 0.0 collective-permute-start.1
  6.3 0.0 copy-done.3
  6.3 0.0 copy-done.4
  6.3 6.2 %shard_map.56 = (f32[4,64,1536]{2,1,0:T(8,128)S(1)}, bf16[1280,64]{1,0:T(8,128)(2,1)S(1)}, bf16[1536,256]{1,0:T(8,128)(2,1)S(1)}, bf16[8,12,16,128]{3,2,1,0:T(8,128)(2,1)S(1)}) custom-call(bf16[5,5,16,64]{3,2,1,0:T(8,128)(2,1)S(1)} %bitcast.7, f32[1,64]{1,0:T(1,128)S(1)} %bitcast.8, bf16[512,1536]{1,0:T(8,128)(2,1)S(1)} %get-tuple-element.12.refs_2_.refs_0_), custom_call_target="tpu_custom_call" | custom-call | flops 1006632960 | bytes 4540672 | tf_op jit(solution)/shard_map/pallas_call | solution.py:45
  12.4 0.7 %collective-permute-done.2.refs_3_ = bf16[96,1536]{1,0:T(8,128)(2,1)S(1)} collective-permute-done((bf16[96,1536]{1,0:T(8,128)(2,1)S(1)}, bf16[96,1536]{1,0:T(8,128)(2,1)S(1)}, u32[]{:S(2)}, u32[]{:S(2)}) %collective-permute-start.2) | collective-permute-done | bytes 294944 | tf_op jit(solution)/shard_map/ppermute | solution.py:472
  13.1 0.0 collective-permute-done.refs_2_
  13.1 1.9 %shard_map.58.refs_6_ = bf16[4,48,1536]{2,1,0:T(8,128)(2,1)S(1)} custom-call(bf16[1280,64]{1,0:T(8,128)(2,1)S(1)} %get-tuple-element.13.refs_0_, f32[4,64,1536]{2,1,0:T(8,128)S(1)} %get-tuple-element.14.refs_1_, bf16[128,1536]{1,0:T(8,128)(2,1)S(1)} %collective-permute-done.refs_2_, bf16[96,1536]{1,0:T(8,128)(2,1)S(1)} %collective-permute-done.2.refs_3_), custom_call_target="tpu_custom_call" | custom-call | flops 62914560 | bytes 3014656 | tf_op jit(solution)/shard_map/pallas_call | solution.py:45
  15.0 0.0 collective-permute-done.1.refs_3_
  15.1 0.0 copy-start.1
  15.1 0.0 copy-start.2
  15.1 1.9 %shard_map.59 = bf16[8,16,16,128]{3,2,1,0:T(8,128)(2,1)} custom-call(bf16[1280,64]{1,0:T(8,128)(2,1)S(1)} %get-tuple-element.13.refs_0_, f32[4,64,1536]{2,1,0:T(8,128)S(1)} %get-tuple-element.14.refs_1_, bf16[128,1536]{1,0:T(8,128)(2,1)S(1)} %collective-permute-done.refs_2_, bf16[32,1536]{1,0:T(8,128)(2,1)S(1)} %collective-permute-done.1.refs_3_, ...), custom_call_target="tpu_custom_call" | custom-call | flops 62914560 | bytes 4521984 | tf_op jit(solution)/shard_map/pallas_call | solution.py:45
  17.0 4.2 %all-to-all-start = ((bf16[8,16,16,128]{3,2,1,0:T(8,128)(2,1)}), bf16[8,16,16,128]{3,2,1,0:T(8,128)(2,1)}, u32[]{:S(2)}, u32[]{:S(2)}) async-start(bf16[8,16,16,128]{3,2,1,0:T(8,128)(2,1)} %shard_map.59), calls=%async_computation | async-start | bytes 1048576 | tf_op jit(solution)/shard_map/all_to_all | solution.py:530
  21.3 0.0 copy-done.1
  21.3 0.0 copy-done.2
  21.3 3.2 %shard_map.60.refs_1_ = bf16[16,768,128]{2,1,0:T(8,128)(2,1)S(1)} custom-call(f32[4,16]{1,0:T(4,128)S(1)} %pad_maximum_fusion.refs_0_, f32[3,8,128]{2,1,0:T(8,128)S(1)} %copy-done.2, bf16[5,5,16,64]{3,2,1,0:T(8,128)(2,1)S(1)} %bitcast.6), custom_call_target="tpu_custom_call" | custom-call | flops 20971520 | bytes 3209472 | tf_op jit(solution)/shard_map/pallas_call | solution.py:45
  24.5 6.5 %all-to-all-done.refs_0_ = bf16[8,16,16,128]{3,2,1,0:T(8,128)(2,1)} async-done(((bf16[8,16,16,128]{3,2,1,0:T(8,128)(2,1)}), bf16[8,16,16,128]{3,2,1,0:T(8,128)(2,1)}, u32[]{:S(2)}, u32[]{:S(2)}) %all-to-all-start) | async-done | bytes 524320 | tf_op jit(solution)/shard_map/all_to_all | solution.py:530
  31.0 4.2 %shard_map.61 = f32[16,2,128,128]{3,2,1,0:T(8,128)} custom-call(bf16[8,16,16,128]{3,2,1,0:T(8,128)(2,1)} %all-to-all-done.refs_0_, bf16[16,768,128]{2,1,0:T(8,128)(2,1)S(1)} %shard_map.60.refs_1_), custom_call_target="tpu_custom_call" | custom-call | flops 268435456 | bytes 5767168 | tf_op jit(solution)/shard_map/pallas_call | solution.py:45
  (3 shorter events, 0.1 us)
Async XLA Ops:
  0.0 1.4 %copy-start = (bf16[64,8,1536]{2,1,0:T(8,128)(2,1)S(1)}, bf16[64,8,1536]{2,1,0:T(8,128)(2,1)}, u32[]{:S(2)}) copy-start(bf16[64,8,1536]{2,1,0:T(8,128)(2,1)} %param.5) | copy-start | bytes 4718596
  1.4 4.8 %copy-start.3 = (bf16[64,16,5,5]{0,1,3,2:T(8,128)(2,1)S(1)}, bf16[64,16,5,5]{0,1,3,2:T(8,128)(2,1)}, u32[]{:S(2)}) copy-start(bf16[64,16,5,5]{0,1,3,2:T(8,128)(2,1)} %param.6) | copy-start | bytes 153604
  1.4 4.8 %copy-start.4 = (f32[64]{0:T(128)S(1)}, f32[64]{0:T(128)}, u32[]{:S(2)}) copy-start(f32[64]{0:T(128)} %param.7) | copy-start | bytes 772
  2.1 11.0 %collective-permute-start = (bf16[128,1536]{1,0:T(8,128)(2,1)S(1)}, bf16[128,1536]{1,0:T(8,128)(2,1)S(1)}, u32[]{:S(2)}, u32[]{:S(2)}) collective-permute-start(bf16[128,1536]{1,0:T(8,128)(2,1)S(1)} %shard_map.57), channel_id=1, source_target_pairs={{0,4},{4,0},{8,12},{12,8},{16,20},{20,16},{24,28},{28,24},{1,5},{5... | collective-permute-start | bytes 1179656 | tf_op jit(solution)/shard_map/ppermute | solution.py:482
  2.7 10.4 %collective-permute-start.2 = (bf16[96,1536]{1,0:T(8,128)(2,1)S(1)}, bf16[96,1536]{1,0:T(8,128)(2,1)S(1)}, u32[]{:S(2)}, u32[]{:S(2)}) collective-permute-start(bf16[96,1536]{1,0:T(8,128)(2,1)S(1)} %get-tuple-element.18), channel_id=1, source_target_pairs={{0,28},{4,8},{8,4},{12,16},{16,12},{20,24},{24,20},{28,0},{1,29},{... | collective-permute-start | bytes 884744 | tf_op jit(solution)/shard_map/ppermute | solution.py:472
  6.2 8.8 %collective-permute-start.1 = (bf16[32,1536]{1,0:T(8,128)(2,1)S(1)}, bf16[32,1536]{1,0:T(8,128)(2,1)S(1)}, u32[]{:S(2)}, u32[]{:S(2)}) collective-permute-start(bf16[32,1536]{1,0:T(8,128)(2,1)S(1)} %get-tuple-element.15), channel_id=1, source_target_pairs={{0,28},{4,8},{8,4},{12,16},{16,12},{20,24},{24,20},{28,0},{1,29},{... | collective-permute-start | bytes 294920 | tf_op jit(solution)/shard_map/ppermute | solution.py:472
  15.1 6.2 %copy-start.1 = (bf16[64,16,5,5]{0,1,3,2:T(8,128)(2,1)S(1)}, bf16[64,16,5,5]{0,1,3,2:T(8,128)(2,1)}, u32[]{:S(2)}) copy-start(bf16[64,16,5,5]{0,1,3,2:T(8,128)(2,1)} %param.8) | copy-start | bytes 153604
  15.1 6.2 %copy-start.2 = (f32[3,8,128]{2,1,0:T(8,128)S(1)}, f32[3,8,128]{2,1,0:T(8,128)}, u32[]{:S(2)}) copy-start(f32[3,8,128]{2,1,0:T(8,128)} %constant.17.clone.refs_1_) | copy-start | bytes 36868
  17.0 14.0 %all-to-all-start = ((bf16[8,16,16,128]{3,2,1,0:T(8,128)(2,1)}), bf16[8,16,16,128]{3,2,1,0:T(8,128)(2,1)}, u32[]{:S(2)}, u32[]{:S(2)}) async-start(bf16[8,16,16,128]{3,2,1,0:T(8,128)(2,1)} %shard_map.59), calls=%async_computation | async-start | bytes 1048576 | tf_op jit(solution)/shard_map/all_to_all | solution.py:530

commit v7 on v5

--- a/solution.py
+++ b/solution.py
@@ -246,35 +246,39 @@
     lax.fori_loop(0, groups[1] - groups[0], per_group, 0)
 
 
-def first_rim_kernel(group, radius, groups, rim_ref, edge_ref, pair_ref, cross_ref, hidden_ref, partial_ref):
+def first_rim_kernel(
+    group, radius, groups, rim_ref, edge_ref, pair_ref, cross_ref, fourier_ref, found_ref, partial_ref, hidden_ref
+):
+    size = found_ref.shape[1]
+
     def store(place, g, at, value):
-        hidden_ref[place, pl.ds(pl.multiple_of(at * group, 16), group), :] = value
+        hidden_ref[pl.ds(pl.multiple_of(place * size + at * group, 16), group), :] = value
 
     write_rim(group, radius, groups, rim_ref, edge_ref, pair_ref, cross_ref, partial_ref, store)
+    found = dot_nn(hidden_ref[...], fourier_ref[...])
+    for place in range(2 * radius):
+        found_ref[place] = found[place * size : (place + 1) * size, :]
 
 
 def last_rim_kernel(
     group, radius, groups, rim_ref, edge_ref, pair_ref, cross_ref, fourier_ref, early_ref, *refs
 ):
     before_refs, (send_hbm, partial_ref, hidden_ref, late_ref, semaphores) = refs[:-5], refs[-5:]
-    channels = edge_ref.shape[1]
     orders = fourier_ref.shape[1] // 2
     early = early_ref.shape[1]
     first = pltpu.make_async_copy(early_ref, send_hbm.at[:, pl.ds(0, early)], semaphores.at[0])
     first.start()
-    for place in range(2 * radius):
-        for before_ref in before_refs:
-            size = before_ref.shape[1]
-            hidden_ref[place * channels : place * channels + size, :] = before_ref[place]
+    size = hidden_ref.shape[0] // (2 * radius)
 
     def store(place, g, at, value):
-        start = pl.multiple_of(place * channels + g * group, 16)
+        start = pl.multiple_of(place * size + at * group, 16)
         hidden_ref[pl.ds(start, group), :] = value
 
     write_rim(group, radius, groups, rim_ref, edge_ref, pair_ref, cross_ref, partial_ref, store)
     found = dot_nn(hidden_ref[...], fourier_ref[...])
     for row in range(2 * radius):
-        mine = found[row * channels : (row + 1) * channels, :]
+        mine = [before_ref[row] for before_ref in before_refs] + [found[row * size : (row + 1) * size, :]]
+        mine = jnp.concatenate(mine, axis=0)
         write_spectra(late_ref, row, mine[:, :orders], mine[:, orders:])
     last = pltpu.make_async_copy(late_ref, send_hbm.at[:, pl.ds(early, 2 * radius)], semaphores.at[1])
     last.start()
@@ -505,11 +509,11 @@
     before = [
         call(
             lambda *refs: first_rim_kernel(group, radius, (0, groups - share), *refs),
-            shapes((2 * radius, (groups - share) * group, length), BF16),
-            [partial],
+            shapes((2 * radius, (groups - share) * group, 2 * ORDERS), F32),
+            [partial, pltpu.VMEM((2 * radius * (groups - share) * group, length), BF16)],
             6,
             flops,
-            (rim, edge, pair, cross),
+            (rim, edge, pair, cross, fourier),
         )
         for cross in crossed[:-1]
     ]
@@ -518,7 +522,7 @@
         shapes((members, 2 * height, owned, wide), BF16),
         [
             partial,
-            pltpu.VMEM((2 * radius * channels, length), BF16),
+            pltpu.VMEM((2 * radius * share * group, length), BF16),
             pltpu.VMEM((members, 2 * radius, owned, wide), BF16),
             pltpu.SemaphoreType.DMA((2,)),
         ],

time: 35.7 us -> 35.7 us (level)
  transfers between devices with their start and end apart: 4 -> 4, of which waited for: 2 -> 2; matrix products, arithmetic and copies ran while one was open for 0% -> 0% of each run, Pallas kernels for 32% -> 33%
where the time goes in v7:
time: 35.7 us; the launch traced here: 35.5 us
  Pallas kernels  18.3 us (51%)
  starting transfers between devices  8.3 us (23%)
  waiting for transfers between devices  7.18 us (20%)
  local copies, waits for them, and re-layouts  1.43 us (4%)
    pallas_call x7, Pallas kernels, call(): pl.pallas_call(kernel, out_shape=out_shape, in_specs=in_specs or [VMEM] *...  18.3 us
    all_to_all x1, waiting for transfers between devices, per_device(): got = lax.all_to_all(send, 'lat', 0, 0, tiled=True)  6.55 us
    all_to_all x1, starting transfers between devices, per_device(): got = lax.all_to_all(send, 'lat', 0, 0, tiled=True)  4.16 us
    ppermute x2, starting transfers between devices, per_device(): crossed[at] = lax.ppermute(cross, 'lat', crosses)  3.58 us
    unnamed x10, local copies, waits for them, and re-layouts  1.43 us
  transfers between devices with their start and end apart: 4, of which 2 were waited for; matrix products, arithmetic and copies ran while one was open for 0% of the time, Pallas kernels for 33%

profile of v7, /device:TPU:0, one launch (start us, length us, event | category | flops | bytes accessed | tf_op | source)
XLA Modules:
  0.0 35.5 jit_solution(9175823573923436986)
XLA Ops:
  0.0 0.0 copy-start
  0.0 1.4 %copy-done = bf16[64,8,1536]{2,1,0:T(8,128)(2,1)S(1)} copy-done((bf16[64,8,1536]{2,1,0:T(8,128)(2,1)S(1)}, bf16[64,8,1536]{2,1,0:T(8,128)(2,1)}, u32[]{:S(2)}) %copy-start) | copy-done | bytes 1572888
  1.4 0.0 copy-start.3
  1.4 0.0 copy-start.4
  1.4 0.3 shard_map.55
  1.8 0.3 shard_map.57
  2.1 0.6 %collective-permute-start = (bf16[128,1536]{1,0:T(8,128)(2,1)S(1)}, bf16[128,1536]{1,0:T(8,128)(2,1)S(1)}, u32[]{:S(2)}, u32[]{:S(2)}) collective-permute-start(bf16[128,1536]{1,0:T(8,128)(2,1)S(1)} %shard_map.57), channel_id=1, source_target_pairs={{0,4},{4,0},{8,12},{12,8},{16,20},{20,16},{24,28},{28,24},{1,5},{5... | collective-permute-start | bytes 1179656 | tf_op jit(solution)/shard_map/ppermute | solution.py:486
  2.7 3.5 %collective-permute-start.2 = (bf16[96,1536]{1,0:T(8,128)(2,1)S(1)}, bf16[96,1536]{1,0:T(8,128)(2,1)S(1)}, u32[]{:S(2)}, u32[]{:S(2)}) collective-permute-start(bf16[96,1536]{1,0:T(8,128)(2,1)S(1)} %get-tuple-element.18), channel_id=1, source_target_pairs={{0,28},{4,8},{8,4},{12,16},{16,12},{20,24},{24,20},{28,0},{1,29},{... | collective-permute-start | bytes 884744 | tf_op jit(solution)/shard_map/ppermute | solution.py:476
  6.2 0.0 collective-permute-start.1
  6.3 0.0 copy-done.3
  6.3 0.0 copy-done.4
  6.3 6.2 %shard_map.56 = (f32[4,64,1536]{2,1,0:T(8,128)S(1)}, bf16[1280,64]{1,0:T(8,128)(2,1)S(1)}, bf16[1536,256]{1,0:T(8,128)(2,1)S(1)}, bf16[8,12,16,128]{3,2,1,0:T(8,128)(2,1)S(1)}) custom-call(bf16[5,5,16,64]{3,2,1,0:T(8,128)(2,1)S(1)} %bitcast.7, f32[1,64]{1,0:T(1,128)S(1)} %bitcast.8, bf16[512,1536]{1,0:T(8,128)(2,1)S(1)} %get-tuple-element.12.refs_2_.refs_0_), custom_call_target="tpu_custom_call" | custom-call | flops 1006632960 | bytes 4540672 | tf_op jit(solution)/shard_map/pallas_call | solution.py:45
  12.5 0.6 %collective-permute-done.2.refs_3_ = bf16[96,1536]{1,0:T(8,128)(2,1)S(1)} collective-permute-done((bf16[96,1536]{1,0:T(8,128)(2,1)S(1)}, bf16[96,1536]{1,0:T(8,128)(2,1)S(1)}, u32[]{:S(2)}, u32[]{:S(2)}) %collective-permute-start.2) | collective-permute-done | bytes 294944 | tf_op jit(solution)/shard_map/ppermute | solution.py:476
  13.1 0.0 collective-permute-done.refs_2_
  13.1 2.2 %shard_map.58.refs_6_ = f32[4,48,256]{2,1,0:T(8,128)S(1)} custom-call(bf16[1280,64]{1,0:T(8,128)(2,1)S(1)} %get-tuple-element.13.refs_0_, f32[4,64,1536]{2,1,0:T(8,128)S(1)} %get-tuple-element.14.refs_1_, bf16[128,1536]{1,0:T(8,128)(2,1)S(1)} %collective-permute-done.refs_2_, bf16[96,1536]{1,0:T(8,128)(2,1)S(1)} %collective-permute-done.2.refs_3_, ...), custom_call_target="tpu_custom_call" | custom-call | flops 62914560 | bytes 3407872 | tf_op jit(solution)/shard_map/pallas_call | solution.py:45
  15.3 0.0 collective-permute-done.1.refs_3_
  15.3 0.0 copy-start.1
  15.4 0.0 copy-start.2
  15.4 1.7 %shard_map.59 = bf16[8,16,16,128]{3,2,1,0:T(8,128)(2,1)} custom-call(bf16[1280,64]{1,0:T(8,128)(2,1)S(1)} %get-tuple-element.13.refs_0_, f32[4,64,1536]{2,1,0:T(8,128)S(1)} %get-tuple-element.14.refs_1_, bf16[128,1536]{1,0:T(8,128)(2,1)S(1)} %collective-permute-done.refs_2_, bf16[32,1536]{1,0:T(8,128)(2,1)S(1)} %collective-permute-done.1.refs_3_, ...), custom_call_target="tpu_custom_call" | custom-call | flops 62914560 | bytes 4128768 | tf_op jit(solution)/shard_map/pallas_call | solution.py:45
  17.0 4.2 %all-to-all-start = ((bf16[8,16,16,128]{3,2,1,0:T(8,128)(2,1)}), bf16[8,16,16,128]{3,2,1,0:T(8,128)(2,1)}, u32[]{:S(2)}, u32[]{:S(2)}) async-start(bf16[8,16,16,128]{3,2,1,0:T(8,128)(2,1)} %shard_map.59), calls=%async_computation | async-start | bytes 1048576 | tf_op jit(solution)/shard_map/all_to_all | solution.py:534
  21.3 0.0 copy-done.1
  21.3 0.0 copy-done.2
  21.3 3.2 %shard_map.60.refs_1_ = bf16[16,768,128]{2,1,0:T(8,128)(2,1)S(1)} custom-call(f32[4,16]{1,0:T(4,128)S(1)} %pad_maximum_fusion.refs_0_, f32[3,8,128]{2,1,0:T(8,128)S(1)} %copy-done.2, bf16[5,5,16,64]{3,2,1,0:T(8,128)(2,1)S(1)} %bitcast.6), custom_call_target="tpu_custom_call" | custom-call | flops 20971520 | bytes 3209472 | tf_op jit(solution)/shard_map/pallas_call | solution.py:45
  24.5 6.5 %all-to-all-done.refs_0_ = bf16[8,16,16,128]{3,2,1,0:T(8,128)(2,1)} async-done(((bf16[8,16,16,128]{3,2,1,0:T(8,128)(2,1)}), bf16[8,16,16,128]{3,2,1,0:T(8,128)(2,1)}, u32[]{:S(2)}, u32[]{:S(2)}) %all-to-all-start) | async-done | bytes 524320 | tf_op jit(solution)/shard_map/all_to_all | solution.py:534
  31.1 4.4 %shard_map.61 = f32[16,2,128,128]{3,2,1,0:T(8,128)} custom-call(bf16[8,16,16,128]{3,2,1,0:T(8,128)(2,1)} %all-to-all-done.refs_0_, bf16[16,768,128]{2,1,0:T(8,128)(2,1)S(1)} %shard_map.60.refs_1_), custom_call_target="tpu_custom_call" | custom-call | flops 268435456 | bytes 5767168 | tf_op jit(solution)/shard_map/pallas_call | solution.py:45
  (3 shorter events, 0.1 us)
Async XLA Ops:
  0.0 1.4 %copy-start = (bf16[64,8,1536]{2,1,0:T(8,128)(2,1)S(1)}, bf16[64,8,1536]{2,1,0:T(8,128)(2,1)}, u32[]{:S(2)}) copy-start(bf16[64,8,1536]{2,1,0:T(8,128)(2,1)} %param.5) | copy-start | bytes 4718596
  1.4 4.8 %copy-start.3 = (bf16[64,16,5,5]{0,1,3,2:T(8,128)(2,1)S(1)}, bf16[64,16,5,5]{0,1,3,2:T(8,128)(2,1)}, u32[]{:S(2)}) copy-start(bf16[64,16,5,5]{0,1,3,2:T(8,128)(2,1)} %param.6) | copy-start | bytes 153604
  1.4 4.8 %copy-start.4 = (f32[64]{0:T(128)S(1)}, f32[64]{0:T(128)}, u32[]{:S(2)}) copy-start(f32[64]{0:T(128)} %param.7) | copy-start | bytes 772
  2.1 11.0 %collective-permute-start = (bf16[128,1536]{1,0:T(8,128)(2,1)S(1)}, bf16[128,1536]{1,0:T(8,128)(2,1)S(1)}, u32[]{:S(2)}, u32[]{:S(2)}) collective-permute-start(bf16[128,1536]{1,0:T(8,128)(2,1)S(1)} %shard_map.57), channel_id=1, source_target_pairs={{0,4},{4,0},{8,12},{12,8},{16,20},{20,16},{24,28},{28,24},{1,5},{5... | collective-permute-start | bytes 1179656 | tf_op jit(solution)/shard_map/ppermute | solution.py:486
  2.7 10.4 %collective-permute-start.2 = (bf16[96,1536]{1,0:T(8,128)(2,1)S(1)}, bf16[96,1536]{1,0:T(8,128)(2,1)S(1)}, u32[]{:S(2)}, u32[]{:S(2)}) collective-permute-start(bf16[96,1536]{1,0:T(8,128)(2,1)S(1)} %get-tuple-element.18), channel_id=1, source_target_pairs={{0,28},{4,8},{8,4},{12,16},{16,12},{20,24},{24,20},{28,0},{1,29},{... | collective-permute-start | bytes 884744 | tf_op jit(solution)/shard_map/ppermute | solution.py:476
  6.2 9.1 %collective-permute-start.1 = (bf16[32,1536]{1,0:T(8,128)(2,1)S(1)}, bf16[32,1536]{1,0:T(8,128)(2,1)S(1)}, u32[]{:S(2)}, u32[]{:S(2)}) collective-permute-start(bf16[32,1536]{1,0:T(8,128)(2,1)S(1)} %get-tuple-element.15), channel_id=1, source_target_pairs={{0,28},{4,8},{8,4},{12,16},{16,12},{20,24},{24,20},{28,0},{1,29},{... | collective-permute-start | bytes 294920 | tf_op jit(solution)/shard_map/ppermute | solution.py:476
  15.3 6.0 %copy-start.1 = (bf16[64,16,5,5]{0,1,3,2:T(8,128)(2,1)S(1)}, bf16[64,16,5,5]{0,1,3,2:T(8,128)(2,1)}, u32[]{:S(2)}) copy-start(bf16[64,16,5,5]{0,1,3,2:T(8,128)(2,1)} %param.8) | copy-start | bytes 153604
  15.4 6.0 %copy-start.2 = (f32[3,8,128]{2,1,0:T(8,128)S(1)}, f32[3,8,128]{2,1,0:T(8,128)}, u32[]{:S(2)}) copy-start(f32[3,8,128]{2,1,0:T(8,128)} %constant.17.clone.refs_1_) | copy-start | bytes 36868
  17.0 14.0 %all-to-all-start = ((bf16[8,16,16,128]{3,2,1,0:T(8,128)(2,1)}), bf16[8,16,16,128]{3,2,1,0:T(8,128)(2,1)}, u32[]{:S(2)}, u32[]{:S(2)}) async-start(bf16[8,16,16,128]{3,2,1,0:T(8,128)(2,1)} %shard_map.59), calls=%async_computation | async-start | bytes 1048576 | tf_op jit(solution)/shard_map/all_to_all | solution.py:534
